TPU v7x, 512 devices: a whole 4x8x8 slice. The times are simulated.
512 devices in a mesh: gx: 16 (over z, y_lo), gy: 16 (over y_hi, x), comp: 2 (over core).
Axes of the slice: x: 4, y: 8 (y_hi: 4, y_lo: 2; y = y_hi * 2 + y_lo), z: 8, core: 2. Of those that a mesh axis runs over, the one named last changes fastest.
Arguments:
- spectrum: bfloat16 [256, 2048, 1024], P('gx', 'gy', 'comp'), may hold values from -6 to 6
- sea_mask: int32 [256, 2048], P('gx', 'gy'), may hold values 0 or 1
- courant: float32 [2, 1024], P(None, 'comp'), may hold values from -0.45 to 0.45
- interaction: bfloat16 [1024, 1024], replicated, may hold values from -0.1875 to 0.1875
- stokes_proj: bfloat16 [2, 1024, 64], replicated, may hold values from -0.1875 to 0.1875
- currents: float32 [2, 64, 256, 2048], P(None, 'comp', 'gx', 'gy'), may hold values from -6 to 6
- level_drag: float32 [64], P('comp'), may hold values from 0.05 to 0.5
Outputs:
- wave_out: bfloat16 [256, 2048, 1024], P('gx', 'gy', 'comp')
- currents_out: float32 [2, 64, 256, 2048], P(None, 'comp', 'gx', 'gy')
All inputs are finite; a program needn't handle non-finite values. No bound on the sum of `sea_mask` on one device may be relied on, other than what follows from the above.
Results may differ from a plain program's by a relative error of at most 0.0049.
Values may be sent and summed in bfloat16 or wider, within the bound.
A program may use at most 64 MiB of HBM per device.

v0:
```python
import jax
import jax.numpy as jnp
from jax import lax
from jax.sharding import PartitionSpec as P

SUBSTEPS = 3


time_step = 0.5
viscosity = 0.4


def padded_2(block, sides, width, periodic):
    for axis, dim in sides:
        count = lax.axis_size(axis)
        forward = [(i, i + 1) for i in range(count - 1)]
        if periodic:
            forward.append((count - 1, 0))
        backward = [(target, source) for source, target in forward]
        low = lax.ppermute(
            lax.slice_in_dim(block, block.shape[dim] - width, None, axis=dim), axis, forward
        )
        high = lax.ppermute(lax.slice_in_dim(block, 0, width, axis=dim), axis, backward)
        block = jnp.concatenate([low, block, high], axis=dim)
    return block


def upwind(centre, west_cell, east_cell, south_cell, north_cell, courant):
    cour_x = courant[0]
    cour_y = courant[1]
    return (
        centre
        - jnp.maximum(cour_x, 0.0) * (centre - west_cell)
        - jnp.minimum(cour_x, 0.0) * (east_cell - centre)
        - jnp.maximum(cour_y, 0.0) * (centre - south_cell)
        - jnp.minimum(cour_y, 0.0) * (north_cell - centre)
    )


def substep(u_pad, v_pad, stokes_u, stokes_v, coriolis, sea_cells, level_drag):
    u_mid = u_pad[:, 1:-1, 1:-1]
    v_mid = v_pad[:, 1:-1, 1:-1]
    vorticity = 0.5 * (v_pad[:, 2:, 1:-1] - v_pad[:, :-2, 1:-1]) - 0.5 * (
        u_pad[:, 1:-1, 2:] - u_pad[:, 1:-1, :-2]
    )
    lap_u = (
        u_pad[:, 2:, 1:-1]
        + u_pad[:, :-2, 1:-1]
        + u_pad[:, 1:-1, 2:]
        + u_pad[:, 1:-1, :-2]
        - 4.0 * u_mid
    )
    lap_v = (
        v_pad[:, 2:, 1:-1]
        + v_pad[:, :-2, 1:-1]
        + v_pad[:, 1:-1, 2:]
        + v_pad[:, 1:-1, :-2]
        - 4.0 * v_mid
    )
    abs_vort = coriolis + vorticity
    drag_col = level_drag[:, None, None]
    u_next = u_mid + time_step * (
        abs_vort * (v_mid + stokes_v) - drag_col * u_mid + viscosity * lap_u
    )
    v_next = v_mid + time_step * (
        -abs_vort * (u_mid + stokes_u) - drag_col * v_mid + viscosity * lap_v
    )
    return (u_next * sea_cells, v_next * sea_cells)


def lat_coriolis(cells_y, margin):
    ny_total = lax.axis_size("gy") * cells_y
    lat_index = lax.axis_index("gy") * cells_y + jnp.arange(-margin, cells_y + margin)
    return jnp.sin(jnp.pi * ((lat_index.astype(jnp.float32) + 0.5) / ny_total - 0.5))[None, :]


def local(spectrum, sea_mask, courant, interaction, stokes_proj, currents, level_drag):
    sea_cells = sea_mask.astype(jnp.float32)
    lon_padded = padded_2(spectrum, (("gx", 0),), 1, True)
    padded = padded_2(lon_padded, (("gy", 1),), 1, False)
    centre = padded[1:-1, 1:-1].astype(jnp.float32)
    west_cell = padded[:-2, 1:-1].astype(jnp.float32)
    east_cell = padded[2:, 1:-1].astype(jnp.float32)
    south_cell = padded[1:-1, :-2].astype(jnp.float32)
    north_cell = padded[1:-1, 2:].astype(jnp.float32)
    advected = (
        upwind(centre, west_cell, east_cell, south_cell, north_cell, courant)
        * sea_cells[:, :, None]
    ).astype(jnp.bfloat16)
    cells_x, cells_y, bins_own = advected.shape
    lev_own = currents.shape[1]
    core_index = lax.axis_index("comp")
    w_cols = lax.dynamic_slice_in_dim(interaction, core_index * bins_own, bins_own, 1)
    proj_own = lax.dynamic_slice_in_dim(stokes_proj, core_index * lev_own, lev_own, 2)
    block_piece = lax.all_gather(advected, "comp", axis=2, tiled=True)
    count = block_piece.shape[2]
    flat_rows = block_piece.reshape(-1, count)
    gain_sum = jnp.dot(flat_rows, w_cols, preferred_element_type=jnp.float32)
    stokes_sum = jnp.einsum(
        "xyk,ckl->clxy", block_piece, proj_own, preferred_element_type=jnp.float32
    )
    wave_out = (
        (advected.astype(jnp.float32) + gain_sum.reshape(cells_x, cells_y, bins_own))
        * sea_cells[:, :, None]
    ).astype(jnp.bfloat16)
    coriolis = lat_coriolis(cells_y, 0)
    flow = currents.reshape(2 * lev_own, cells_x, cells_y)
    for sub_index in range(SUBSTEPS):
        lon_flow = padded_2(flow, (("gx", 1),), 1, True)
        full_flow = padded_2(lon_flow, (("gy", 2),), 1, False)
        u_next, v_next = substep(
            full_flow[:lev_own],
            full_flow[lev_own:],
            stokes_sum[0],
            stokes_sum[1],
            coriolis,
            sea_cells,
            level_drag,
        )
        flow = jnp.concatenate([u_next, v_next], 0)
    currents_out = flow.reshape(2, lev_own, cells_x, cells_y)
    return (wave_out, currents_out)


def solution(mesh):
    in_specs = (
        P("gx", "gy", "comp"),
        P("gx", "gy"),
        P(None, "comp"),
        P(),
        P(),
        P(None, "comp", "gx", "gy"),
        P("comp"),
    )
    out_specs = (P("gx", "gy", "comp"), P(None, "comp", "gx", "gy"))
    return jax.shard_map(local, mesh=mesh, in_specs=in_specs, out_specs=out_specs, check_vma=False)
```

profile of v0, /device:TPU:168, one launch (start us, length us, event | category | flops | bytes accessed | tf_op | source)
XLA Modules:
  0.0 161.8 jit_solution(15437891805474888533)
XLA Ops:
  8.4 5.2 %collective-permute-start = (bf16[1,128,512]{2,1,0:T(8,128)(2,1)S(1)}, bf16[1,128,512]{2,1,0:T(8,128)(2,1)S(1)}, u32[]{:S(2)}, u32[]{:S(2)}) collective-permute-start(bf16[1,128,512]{2,1,0:T(8,128)(2,1)S(1)} %get-tuple-element.9), channel_id=1, source_target_pairs={{0,32},{32,64},{64,96},{96,128},{128,160},{160,192},{192,224},{224... | collective-permute-start | bytes 393224 | tf_op jit(solution)/shard_map/ppermute | solution.py:20
  13.6 1.9 %collective-permute-start.1 = (bf16[1,128,512]{2,1,0:T(8,128)(2,1)S(1)}, bf16[1,128,512]{2,1,0:T(8,128)(2,1)S(1)}, u32[]{:S(2)}, u32[]{:S(2)}) collective-permute-start(bf16[1,128,512]{2,1,0:T(8,128)(2,1)S(1)} %get-tuple-element.8), channel_id=1, source_target_pairs={{32,0},{64,32},{96,64},{128,96},{160,128},{192,160},{224,192},{256... | collective-permute-start | bytes 393224 | tf_op jit(solution)/shard_map/ppermute | solution.py:23
  15.5 1.7 %collective-permute-done = bf16[1,128,512]{2,1,0:T(8,128)(2,1)S(1)} collective-permute-done((bf16[1,128,512]{2,1,0:T(8,128)(2,1)S(1)}, bf16[1,128,512]{2,1,0:T(8,128)(2,1)S(1)}, u32[]{:S(2)}, u32[]{:S(2)}) %collective-permute-start) | collective-permute-done | bytes 131104 | tf_op jit(solution)/shard_map/ppermute | solution.py:20
  17.2 1.8 %constant_dynamic-update-slice_fusion.1 = bf16[18,128,512]{2,1,0:T(8,128)(2,1)S(1)} fusion(bf16[18,128,512]{2,1,0:T(8,128)(2,1)S(1)} %constant_dynamic-update-slice_fusion.2, bf16[16,128,512]{2,1,0:T(8,128)(2,1)} %param.7), kind=kLoop, calls=%fused_computation.136 | loop fusion | bytes 4194304
  19.0 2.3 %collective-permute-done.1 = bf16[1,128,512]{2,1,0:T(8,128)(2,1)S(1)} collective-permute-done((bf16[1,128,512]{2,1,0:T(8,128)(2,1)S(1)}, bf16[1,128,512]{2,1,0:T(8,128)(2,1)S(1)}, u32[]{:S(2)}, u32[]{:S(2)}) %collective-permute-start.1) | collective-permute-done | bytes 131104 | tf_op jit(solution)/shard_map/ppermute | solution.py:23
  21.4 3.4 %collective-permute-start.2 = (bf16[18,1,512]{2,1,0:T(2,128)(2,1)S(1)}, bf16[18,1,512]{2,1,0:T(2,128)(2,1)S(1)}, u32[]{:S(2)}, u32[]{:S(2)}) collective-permute-start(bf16[18,1,512]{2,1,0:T(2,128)(2,1)S(1)} %get-tuple-element.6), channel_id=1, source_target_pairs={{0,2},{2,4},{4,6},{6,8},{8,10},{10,12},{12,14},{14,16},{16,18},{18... | collective-permute-start | bytes 55304 | tf_op jit(solution)/shard_map/ppermute | solution.py:20
  24.9 6.7 %collective-permute-start.3 = (bf16[18,1,512]{2,1,0:T(2,128)(2,1)S(1)}, bf16[18,1,512]{2,1,0:T(2,128)(2,1)S(1)}, u32[]{:S(2)}, u32[]{:S(2)}) collective-permute-start(bf16[18,1,512]{2,1,0:T(2,128)(2,1)S(1)} %get-tuple-element.7), channel_id=1, source_target_pairs={{2,0},{4,2},{6,4},{8,6},{10,8},{12,10},{14,12},{16,14},{18,16},{20... | collective-permute-start | bytes 55304 | tf_op jit(solution)/shard_map/ppermute | solution.py:23
  31.6 1.5 collective-permute-done.3
  33.1 7.7 %fusion.5 = bf16[16,128,512]{2,1,0:T(8,128)(2,1)} fusion(bf16[16,128,512]{2,1,0:T(8,128)(2,1)S(1)} %copy-done.1, bf16[18,1,512]{2,1,0:T(2,128)(2,1)S(1)} %collective-permute-done.3, bf16[18,128,512]{2,1,0:T(8,128)(2,1)S(1)} %constant_dynamic-update-slice_fusion, bf16[18,1,512]{2,1,0:T(2,128)(2,1)S(1)} %collective-permute-done.2, ...), kind=kLoop, calls=%fused_computation.10 | loop fusion | flops 32505856 | bytes 6868992 | tf_op jit(solution)/shard_map/convert_element_type | solution.py:89
  41.1 5.2 %collective-permute-start.5 = (f32[64,1,128]{2,0,1:T(8,128)S(1)}, f32[64,1,128]{2,0,1:T(8,128)S(1)}, u32[]{:S(2)}, u32[]{:S(2)}) collective-permute-start(f32[64,1,128]{2,0,1:T(8,128)S(1)} %get-tuple-element.22), channel_id=1, source_target_pairs={{0,32},{32,64},{64,96},{96,128},{128,160},{160,192},{192,224},{224... | collective-permute-start | bytes 98312 | tf_op jit(solution)/shard_map/ppermute | solution.py:20
  46.3 1.9 %collective-permute-start.4 = (f32[64,1,128]{2,0,1:T(8,128)S(1)}, f32[64,1,128]{2,0,1:T(8,128)S(1)}, u32[]{:S(2)}, u32[]{:S(2)}) collective-permute-start(f32[64,1,128]{2,0,1:T(8,128)S(1)} %get-tuple-element.23), channel_id=1, source_target_pairs={{32,0},{64,32},{96,64},{128,96},{160,128},{192,160},{224,192},{256... | collective-permute-start | bytes 98312 | tf_op jit(solution)/shard_map/ppermute | solution.py:23
  49.1 4.0 %collective-permute-done.4 = f32[64,1,128]{2,0,1:T(8,128)S(1)} collective-permute-done((f32[64,1,128]{2,0,1:T(8,128)S(1)}, f32[64,1,128]{2,0,1:T(8,128)S(1)}, u32[]{:S(2)}, u32[]{:S(2)}) %collective-permute-start.4) | collective-permute-done | bytes 32800 | tf_op jit(solution)/shard_map/ppermute | solution.py:23
  57.0 1.9 %collective-permute-start.7 = (f32[64,18,1]{0,2,1:T(1,128)S(1)}, f32[64,18,1]{0,2,1:T(1,128)S(1)}, u32[]{:S(2)}, u32[]{:S(2)}) collective-permute-start(f32[64,18,1]{0,2,1:T(1,128)S(1)} %copy.17), channel_id=1, source_target_pairs={{0,2},{2,4},{4,6},{6,8},{8,10},{10,12},{12,14},{14,16},{16,18},{18... | collective-permute-start | bytes 13832 | tf_op jit(solution)/shard_map/ppermute | solution.py:20
  58.9 8.6 %collective-permute-start.6 = (f32[64,18,1]{0,2,1:T(1,128)S(1)}, f32[64,18,1]{0,2,1:T(1,128)S(1)}, u32[]{:S(2)}, u32[]{:S(2)}) collective-permute-start(f32[64,18,1]{0,2,1:T(1,128)S(1)} %copy.15), channel_id=1, source_target_pairs={{2,0},{4,2},{6,4},{8,6},{10,8},{12,10},{14,12},{16,14},{18,16},{20... | collective-permute-start | bytes 13832 | tf_op jit(solution)/shard_map/ppermute | solution.py:23
  71.1 3.7 %fusion.9 = f32[2,32,16,128]{3,1,2,0:T(8,128)S(1)} fusion(bf16[16,128,1024]{2,1,0:T(8,128)(2,1)} %all-gather.2.cloned.1.call-done, bf16[2,1024,64]{1,2,0:T(8,128)(2,1)S(1)} %copy-done.9, s32[]{:T(128)S(6)} %select_n.7), kind=kOutput, calls=%fused_computation.14 | convolution fusion | flops 268435456 | bytes 4849668 | tf_op jit(solution)/shard_map/xyk,ckl->clxy/dot_general | solution.py:99
  74.8 1.6 fusion.53
  76.4 1.4 fusion.63
  77.8 3.9 %collective-permute-start.9 = (f32[64,1,128]{2,0,1:T(8,128)S(1)}, f32[64,1,128]{2,0,1:T(8,128)S(1)}, u32[]{:S(2)}, u32[]{:S(2)}) collective-permute-start(f32[64,1,128]{2,0,1:T(8,128)S(1)} %get-tuple-element.18), channel_id=1, source_target_pairs={{0,32},{32,64},{64,96},{96,128},{128,160},{160,192},{192,224},{224... | collective-permute-start | bytes 98312 | tf_op jit(solution)/shard_map/ppermute | solution.py:20
  81.8 1.9 %collective-permute-start.8 = (f32[64,1,128]{2,0,1:T(8,128)S(1)}, f32[64,1,128]{2,0,1:T(8,128)S(1)}, u32[]{:S(2)}, u32[]{:S(2)}) collective-permute-start(f32[64,1,128]{2,0,1:T(8,128)S(1)} %get-tuple-element.19), channel_id=1, source_target_pairs={{32,0},{64,32},{96,64},{128,96},{160,128},{192,160},{224,192},{256... | collective-permute-start | bytes 98312 | tf_op jit(solution)/shard_map/ppermute | solution.py:23
  83.7 5.4 %collective-permute-done.8 = f32[64,1,128]{2,0,1:T(8,128)S(1)} collective-permute-done((f32[64,1,128]{2,0,1:T(8,128)S(1)}, f32[64,1,128]{2,0,1:T(8,128)S(1)}, u32[]{:S(2)}, u32[]{:S(2)}) %collective-permute-start.8) | collective-permute-done | bytes 32800 | tf_op jit(solution)/shard_map/ppermute | solution.py:23
  91.7 8.4 %collective-permute-start.10 = (f32[64,18,1]{0,2,1:T(1,128)S(1)}, f32[64,18,1]{0,2,1:T(1,128)S(1)}, u32[]{:S(2)}, u32[]{:S(2)}) collective-permute-start(f32[64,18,1]{0,2,1:T(1,128)S(1)} %copy.20), channel_id=1, source_target_pairs={{2,0},{4,2},{6,4},{8,6},{10,8},{12,10},{14,12},{16,14},{18,16},{20... | collective-permute-start | bytes 13832 | tf_op jit(solution)/shard_map/ppermute | solution.py:23
  101.4 1.9 %collective-permute-start.11 = (f32[64,18,1]{0,2,1:T(1,128)S(1)}, f32[64,18,1]{0,2,1:T(1,128)S(1)}, u32[]{:S(2)}, u32[]{:S(2)}) collective-permute-start(f32[64,18,1]{0,2,1:T(1,128)S(1)} %copy.22), channel_id=1, source_target_pairs={{0,2},{2,4},{4,6},{6,8},{8,10},{10,12},{12,14},{14,16},{16,18},{18... | collective-permute-start | bytes 13832 | tf_op jit(solution)/shard_map/ppermute | solution.py:20
  104.5 6.7 %collective-permute-done.11 = f32[64,18,1]{0,2,1:T(1,128)S(1)} collective-permute-done((f32[64,18,1]{0,2,1:T(1,128)S(1)}, f32[64,18,1]{0,2,1:T(1,128)S(1)}, u32[]{:S(2)}, u32[]{:S(2)}) %collective-permute-start.11) | collective-permute-done | bytes 4640 | tf_op jit(solution)/shard_map/ppermute | solution.py:20
  112.3 1.3 fusion.46
  113.6 1.7 %fusion.36 = f32[32,16,128]{2,0,1:T(8,128)S(1)} fusion(f32[32,16,128]{2,0,1:T(8,128)S(1)} %fusion.53, f32[64,18,1]{2,0,1:T(8,128)} %copy.23, f32[64,1,128]{2,0,1:T(8,128)S(1)} %collective-permute-done.8, f32[64,1,128]{2,0,1:T(8,128)S(1)} %collective-permute-done.9, f32[32,16,128]{2,0,1:T(8,128)S(1)} %copy-done.3, f32[64,18,1]{2,0,1:T(8,128)} %copy.21, ...), kind=kLoop, calls=%fused_computation.67 | loop fusion | flops 2686976 | bytes 1132160 | tf_op jit(solution)/shard_map/mul | solution.py:68
  116.1 3.9 %collective-permute-start.13 = (f32[64,1,128]{2,0,1:T(8,128)S(1)}, f32[64,1,128]{2,0,1:T(8,128)S(1)}, u32[]{:S(2)}, u32[]{:S(2)}) collective-permute-start(f32[64,1,128]{2,0,1:T(8,128)S(1)} %get-tuple-element.16), channel_id=1, source_target_pairs={{0,32},{32,64},{64,96},{96,128},{128,160},{160,192},{192,224},{224... | collective-permute-start | bytes 98312 | tf_op jit(solution)/shard_map/ppermute | solution.py:20
  120.0 1.9 %collective-permute-start.12 = (f32[64,1,128]{2,0,1:T(8,128)S(1)}, f32[64,1,128]{2,0,1:T(8,128)S(1)}, u32[]{:S(2)}, u32[]{:S(2)}) collective-permute-start(f32[64,1,128]{2,0,1:T(8,128)S(1)} %get-tuple-element.17), channel_id=1, source_target_pairs={{32,0},{64,32},{96,64},{128,96},{160,128},{192,160},{224,192},{256... | collective-permute-start | bytes 98312 | tf_op jit(solution)/shard_map/ppermute | solution.py:23
  121.9 4.8 %collective-permute-done.12 = f32[64,1,128]{2,0,1:T(8,128)S(1)} collective-permute-done((f32[64,1,128]{2,0,1:T(8,128)S(1)}, f32[64,1,128]{2,0,1:T(8,128)S(1)}, u32[]{:S(2)}, u32[]{:S(2)}) %collective-permute-start.12) | collective-permute-done | bytes 32800 | tf_op jit(solution)/shard_map/ppermute | solution.py:23
  131.5 2.1 %collective-permute-start.15 = (f32[64,18,1]{0,2,1:T(1,128)S(1)}, f32[64,18,1]{0,2,1:T(1,128)S(1)}, u32[]{:S(2)}, u32[]{:S(2)}) collective-permute-start(f32[64,18,1]{0,2,1:T(1,128)S(1)} %copy.26), channel_id=1, source_target_pairs={{0,2},{2,4},{4,6},{6,8},{8,10},{10,12},{12,14},{14,16},{16,18},{18... | collective-permute-start | bytes 13832 | tf_op jit(solution)/shard_map/ppermute | solution.py:20
  133.6 8.3 %collective-permute-start.14 = (f32[64,18,1]{0,2,1:T(1,128)S(1)}, f32[64,18,1]{0,2,1:T(1,128)S(1)}, u32[]{:S(2)}, u32[]{:S(2)}) collective-permute-start(f32[64,18,1]{0,2,1:T(1,128)S(1)} %copy.24), channel_id=1, source_target_pairs={{2,0},{4,2},{6,4},{8,6},{10,8},{12,10},{14,12},{16,14},{18,16},{20... | collective-permute-start | bytes 13832 | tf_op jit(solution)/shard_map/ppermute | solution.py:23
  141.9 6.7 %multiply_convert_fusion = bf16[16,128,512]{2,1,0:T(8,128)(2,1)} fusion(bf16[16,128,512]{2,1,0:T(8,128)(2,1)} %fusion.5, f32[16,128]{1,0:T(8,128)S(1)} %convert_element_type.39, bf16[16,128,1024]{2,1,0:T(8,128)(2,1)} %all-gather.2.cloned.1.call-done, bf16[1024,1024]{1,0:T(8,128)(2,1)S(1)} %copy-done, s32[]{:T(128)S(6)} %select_n.6), kind=kOutput, calls=%fused_computation.16 | convolution fusion | flops 2151677952 | bytes 9445380 | tf_op jit(solution)/shard_map/dot_general | solution.py:98
  152.2 1.7 %fusion.19 = f32[32,16,128]{2,0,1:T(8,128)S(1)} fusion(f32[32,16,128]{2,0,1:T(8,128)S(1)} %copy-done.5, f32[64,18,1]{2,0,1:T(8,128)} %copy.27, f32[64,1,128]{2,0,1:T(8,128)S(1)} %collective-permute-done.12, f32[64,1,128]{2,0,1:T(8,128)S(1)} %collective-permute-done.13, f32[32,16,128]{2,0,1:T(8,128)S(1)} %fusion.46, f32[64,18,1]{2,0,1:T(8,128)} %copy.25, ...), kind=kLoop, calls=%fused_computation.34 | loop fusion | flops 2686976 | bytes 1132160 | tf_op jit(solution)/shard_map/mul | solution.py:68
  (71 shorter events, 26.1 us)
Async XLA Ops:
  7.2 134.7 %copy-start = (bf16[1024,1024]{1,0:T(8,128)(2,1)S(1)}, bf16[1024,1024]{1,0:T(8,128)(2,1)}, u32[]{:S(2)}) copy-start(bf16[1024,1024]{1,0:T(8,128)(2,1)} %param.10) | copy-start | bytes 6291460
  7.2 24.3 %copy-start.12 = (f32[2,512]{1,0:T(2,128)S(1)}, f32[2,512]{1,0:T(2,128)}, u32[]{:S(2)}) copy-start(f32[2,512]{1,0:T(2,128)} %param.9) | copy-start | bytes 12292
  7.2 24.4 %copy-start.11 = (s32[16,128]{1,0:T(8,128)S(1)}, s32[16,128]{1,0:T(8,128)}, u32[]{:S(2)}) copy-start(s32[16,128]{1,0:T(8,128)} %param.8) | copy-start | bytes 24580
  7.2 63.9 %all-gather.2.cloned.1.call-start = ((), (), s32[]{:S(2)}) async-start(), calls=%async_computation | async-start | bytes 6291456 | tf_op jit(solution)/shard_map/all_gather | solution.py:95
  7.2 25.9 %copy-start.1 = (bf16[16,128,512]{2,1,0:T(8,128)(2,1)S(1)}, bf16[16,128,512]{2,1,0:T(8,128)(2,1)}, u32[]{:S(2)}) copy-start(bf16[16,128,512]{2,1,0:T(8,128)(2,1)} %param.7) | copy-start | bytes 6291460
  8.4 8.8 %collective-permute-start = (bf16[1,128,512]{2,1,0:T(8,128)(2,1)S(1)}, bf16[1,128,512]{2,1,0:T(8,128)(2,1)S(1)}, u32[]{:S(2)}, u32[]{:S(2)}) collective-permute-start(bf16[1,128,512]{2,1,0:T(8,128)(2,1)S(1)} %get-tuple-element.9), channel_id=1, source_target_pairs={{0,32},{32,64},{64,96},{96,128},{128,160},{160,192},{192,224},{224... | collective-permute-start | bytes 393224 | tf_op jit(solution)/shard_map/ppermute | solution.py:20
  13.6 7.8 %collective-permute-start.1 = (bf16[1,128,512]{2,1,0:T(8,128)(2,1)S(1)}, bf16[1,128,512]{2,1,0:T(8,128)(2,1)S(1)}, u32[]{:S(2)}, u32[]{:S(2)}) collective-permute-start(bf16[1,128,512]{2,1,0:T(8,128)(2,1)S(1)} %get-tuple-element.8), channel_id=1, source_target_pairs={{32,0},{64,32},{96,64},{128,96},{160,128},{192,160},{224,192},{256... | collective-permute-start | bytes 393224 | tf_op jit(solution)/shard_map/ppermute | solution.py:23
  21.4 10.2 %collective-permute-start.2 = (bf16[18,1,512]{2,1,0:T(2,128)(2,1)S(1)}, bf16[18,1,512]{2,1,0:T(2,128)(2,1)S(1)}, u32[]{:S(2)}, u32[]{:S(2)}) collective-permute-start(bf16[18,1,512]{2,1,0:T(2,128)(2,1)S(1)} %get-tuple-element.6), channel_id=1, source_target_pairs={{0,2},{2,4},{4,6},{6,8},{8,10},{10,12},{12,14},{14,16},{16,18},{18... | collective-permute-start | bytes 55304 | tf_op jit(solution)/shard_map/ppermute | solution.py:20
  24.9 8.3 %collective-permute-start.3 = (bf16[18,1,512]{2,1,0:T(2,128)(2,1)S(1)}, bf16[18,1,512]{2,1,0:T(2,128)(2,1)S(1)}, u32[]{:S(2)}, u32[]{:S(2)}) collective-permute-start(bf16[18,1,512]{2,1,0:T(2,128)(2,1)S(1)} %get-tuple-element.7), channel_id=1, source_target_pairs={{2,0},{4,2},{6,4},{8,6},{10,8},{12,10},{14,12},{16,14},{18,16},{20... | collective-permute-start | bytes 55304 | tf_op jit(solution)/shard_map/ppermute | solution.py:23
  33.1 7.8 %copy-start.8 = (f32[2,32,16,128]{3,2,1,0:T(8,128)S(1)}, f32[2,32,16,128]{3,2,1,0:T(8,128)}, u32[]{:S(2)}) copy-start(f32[2,32,16,128]{3,2,1,0:T(8,128)} %param.12) | copy-start | bytes 1572868
  40.9 30.2 %copy-start.9 = (bf16[2,1024,64]{1,2,0:T(8,128)(2,1)S(1)}, bf16[2,1024,64]{1,2,0:T(8,128)(2,1)}, u32[]{:S(2)}) copy-start(bf16[2,1024,64]{1,2,0:T(8,128)(2,1)} %param.11) | copy-start | bytes 786436
  41.1 8.0 %collective-permute-start.5 = (f32[64,1,128]{2,0,1:T(8,128)S(1)}, f32[64,1,128]{2,0,1:T(8,128)S(1)}, u32[]{:S(2)}, u32[]{:S(2)}) collective-permute-start(f32[64,1,128]{2,0,1:T(8,128)S(1)} %get-tuple-element.22), channel_id=1, source_target_pairs={{0,32},{32,64},{64,96},{96,128},{128,160},{160,192},{192,224},{224... | collective-permute-start | bytes 98312 | tf_op jit(solution)/shard_map/ppermute | solution.py:20
  46.3 6.8 %collective-permute-start.4 = (f32[64,1,128]{2,0,1:T(8,128)S(1)}, f32[64,1,128]{2,0,1:T(8,128)S(1)}, u32[]{:S(2)}, u32[]{:S(2)}) collective-permute-start(f32[64,1,128]{2,0,1:T(8,128)S(1)} %get-tuple-element.23), channel_id=1, source_target_pairs={{32,0},{64,32},{96,64},{128,96},{160,128},{192,160},{224,192},{256... | collective-permute-start | bytes 98312 | tf_op jit(solution)/shard_map/ppermute | solution.py:23
  54.4 20.4 %copy-start.10 = (f32[32]{0:T(128)S(1)}, f32[32]{0:T(128)}, u32[]{:S(2)}) copy-start(f32[32]{0:T(128)} %param.13) | copy-start | bytes 388
  57.0 13.0 %collective-permute-start.7 = (f32[64,18,1]{0,2,1:T(1,128)S(1)}, f32[64,18,1]{0,2,1:T(1,128)S(1)}, u32[]{:S(2)}, u32[]{:S(2)}) collective-permute-start(f32[64,18,1]{0,2,1:T(1,128)S(1)} %copy.17), channel_id=1, source_target_pairs={{0,2},{2,4},{4,6},{6,8},{8,10},{10,12},{12,14},{14,16},{16,18},{18... | collective-permute-start | bytes 13832 | tf_op jit(solution)/shard_map/ppermute | solution.py:20
  58.9 10.0 %collective-permute-start.6 = (f32[64,18,1]{0,2,1:T(1,128)S(1)}, f32[64,18,1]{0,2,1:T(1,128)S(1)}, u32[]{:S(2)}, u32[]{:S(2)}) collective-permute-start(f32[64,18,1]{0,2,1:T(1,128)S(1)} %copy.15), channel_id=1, source_target_pairs={{2,0},{4,2},{6,4},{8,6},{10,8},{12,10},{14,12},{16,14},{18,16},{20... | collective-permute-start | bytes 13832 | tf_op jit(solution)/shard_map/ppermute | solution.py:23
  71.1 3.7 %copy-start.6 = (f32[64,18,1]{2,0,1:T(8,128)S(1)}, f32[64,18,1]{2,0,1:T(8,128)}, u32[]{:S(2)}) copy-start(f32[64,18,1]{2,0,1:T(8,128)} %copy.16) | copy-start | bytes 13828
  71.1 3.7 %copy-start.7 = (f32[64,18,1]{2,0,1:T(8,128)S(1)}, f32[64,18,1]{2,0,1:T(8,128)}, u32[]{:S(2)}) copy-start(f32[64,18,1]{2,0,1:T(8,128)} %copy.18) | copy-start | bytes 13828
  77.8 11.3 %copy-start.2 = (f32[32,16,128]{2,0,1:T(8,128)}, f32[32,16,128]{2,0,1:T(8,128)S(1)}, u32[]{:S(2)}) copy-start(f32[32,16,128]{2,0,1:T(8,128)S(1)} %fusion.63) | copy-start | bytes 786436
  77.8 5.9 %collective-permute-start.9 = (f32[64,1,128]{2,0,1:T(8,128)S(1)}, f32[64,1,128]{2,0,1:T(8,128)S(1)}, u32[]{:S(2)}, u32[]{:S(2)}) collective-permute-start(f32[64,1,128]{2,0,1:T(8,128)S(1)} %get-tuple-element.18), channel_id=1, source_target_pairs={{0,32},{32,64},{64,96},{96,128},{128,160},{160,192},{192,224},{224... | collective-permute-start | bytes 98312 | tf_op jit(solution)/shard_map/ppermute | solution.py:20
  81.8 7.4 %collective-permute-start.8 = (f32[64,1,128]{2,0,1:T(8,128)S(1)}, f32[64,1,128]{2,0,1:T(8,128)S(1)}, u32[]{:S(2)}, u32[]{:S(2)}) collective-permute-start(f32[64,1,128]{2,0,1:T(8,128)S(1)} %get-tuple-element.19), channel_id=1, source_target_pairs={{32,0},{64,32},{96,64},{128,96},{160,128},{192,160},{224,192},{256... | collective-permute-start | bytes 98312 | tf_op jit(solution)/shard_map/ppermute | solution.py:23
  89.2 23.1 %copy-start.3 = (f32[32,16,128]{2,0,1:T(8,128)S(1)}, f32[32,16,128]{2,0,1:T(8,128)}, u32[]{:S(2)}) copy-start(f32[32,16,128]{2,0,1:T(8,128)} %copy-done.2) | copy-start | bytes 786436
  91.7 11.6 %collective-permute-start.10 = (f32[64,18,1]{0,2,1:T(1,128)S(1)}, f32[64,18,1]{0,2,1:T(1,128)S(1)}, u32[]{:S(2)}, u32[]{:S(2)}) collective-permute-start(f32[64,18,1]{0,2,1:T(1,128)S(1)} %copy.20), channel_id=1, source_target_pairs={{2,0},{4,2},{6,4},{8,6},{10,8},{12,10},{14,12},{16,14},{18,16},{20... | collective-permute-start | bytes 13832 | tf_op jit(solution)/shard_map/ppermute | solution.py:23
  101.4 9.8 %collective-permute-start.11 = (f32[64,18,1]{0,2,1:T(1,128)S(1)}, f32[64,18,1]{0,2,1:T(1,128)S(1)}, u32[]{:S(2)}, u32[]{:S(2)}) collective-permute-start(f32[64,18,1]{0,2,1:T(1,128)S(1)} %copy.22), channel_id=1, source_target_pairs={{0,2},{2,4},{4,6},{6,8},{8,10},{10,12},{12,14},{14,16},{16,18},{18... | collective-permute-start | bytes 13832 | tf_op jit(solution)/shard_map/ppermute | solution.py:20
  115.3 0.7 copy-start.4
  116.1 5.9 %collective-permute-start.13 = (f32[64,1,128]{2,0,1:T(8,128)S(1)}, f32[64,1,128]{2,0,1:T(8,128)S(1)}, u32[]{:S(2)}, u32[]{:S(2)}) collective-permute-start(f32[64,1,128]{2,0,1:T(8,128)S(1)} %get-tuple-element.16), channel_id=1, source_target_pairs={{0,32},{32,64},{64,96},{96,128},{128,160},{160,192},{192,224},{224... | collective-permute-start | bytes 98312 | tf_op jit(solution)/shard_map/ppermute | solution.py:20
  120.0 6.7 %collective-permute-start.12 = (f32[64,1,128]{2,0,1:T(8,128)S(1)}, f32[64,1,128]{2,0,1:T(8,128)S(1)}, u32[]{:S(2)}, u32[]{:S(2)}) collective-permute-start(f32[64,1,128]{2,0,1:T(8,128)S(1)} %get-tuple-element.17), channel_id=1, source_target_pairs={{32,0},{64,32},{96,64},{128,96},{160,128},{192,160},{224,192},{256... | collective-permute-start | bytes 98312 | tf_op jit(solution)/shard_map/ppermute | solution.py:23
  131.5 19.3 %copy-start.5 = (f32[32,16,128]{2,0,1:T(8,128)S(1)}, f32[32,16,128]{2,0,1:T(8,128)}, u32[]{:S(2)}) copy-start(f32[32,16,128]{2,0,1:T(8,128)} %copy-done.4) | copy-start | bytes 786436
  131.5 18.2 %collective-permute-start.15 = (f32[64,18,1]{0,2,1:T(1,128)S(1)}, f32[64,18,1]{0,2,1:T(1,128)S(1)}, u32[]{:S(2)}, u32[]{:S(2)}) collective-permute-start(f32[64,18,1]{0,2,1:T(1,128)S(1)} %copy.26), channel_id=1, source_target_pairs={{0,2},{2,4},{4,6},{6,8},{8,10},{10,12},{12,14},{14,16},{16,18},{18... | collective-permute-start | bytes 13832 | tf_op jit(solution)/shard_map/ppermute | solution.py:20
  133.6 15.0 %collective-permute-start.14 = (f32[64,18,1]{0,2,1:T(1,128)S(1)}, f32[64,18,1]{0,2,1:T(1,128)S(1)}, u32[]{:S(2)}, u32[]{:S(2)}) collective-permute-start(f32[64,18,1]{0,2,1:T(1,128)S(1)} %copy.24), channel_id=1, source_target_pairs={{2,0},{4,2},{6,4},{8,6},{10,8},{12,10},{14,12},{16,14},{18,16},{20... | collective-permute-start | bytes 13832 | tf_op jit(solution)/shard_map/ppermute | solution.py:23
Sparse Core Ops, SparseCore 0:
  41.0 24.5 all-gather.1
where the time goes:
time: 163 us; the launch traced here: 162 us
  starting transfers between devices  67.3 us (41%)
  waiting for transfers between devices  27.8 us (17%)
  local copies, waits for them, and re-layouts  24 us (15%)
  other arithmetic  17.9 us (11%)
  between operations  14.5 us (9%)
  matrix products  10.4 us (6%)
    ppermute x8, starting transfers between devices, padded_2(): lax.ppermute(lax.slice_in_dim(block, 0, width, axis=dim), axis, backward)  39.7 us
    ppermute x8, starting transfers between devices, padded_2(): lax.ppermute(lax.slice_in_dim(block, block.shape[dim] - width, None, axis...  27.5 us
    ppermute x8, waiting for transfers between devices, padded_2(): lax.ppermute(lax.slice_in_dim(block, 0, width, axis=dim), axis, backward)  19.4 us
    mul x6, other arithmetic, substep(): return (u_next * sea_cells, v_next * sea_cells)  9.03 us
    slice x7, local copies, waits for them, and re-layouts, padded_2(): lax.slice_in_dim(block, 0, width, axis=dim)  8.73 us
    ppermute x8, waiting for transfers between devices, padded_2(): lax.ppermute(lax.slice_in_dim(block, block.shape[dim] - width, None, axis...  8.44 us
    convert_element_type x1, other arithmetic, local(): advected = (upwind(centre, west_cell, east_cell, south_cell, north_cell,...  7.73 us
    dot_general x1, matrix products, local(): gain_sum = jnp.dot(flat_rows, w_cols, preferred_element_type=jnp.float32)  6.69 us
  transfers between devices with their start and end apart: 17, of which 8 were waited for; matrix products, arithmetic and copies ran while one was open for 12% of the time, Pallas kernels for 0%

commit v1 on v0

v1 whole, which is shorter than its diff:
```python
import functools

import jax
import jax.numpy as jnp
from jax import lax
from jax.experimental import pallas as pl
from jax.experimental.pallas import tpu as pltpu
from jax.sharding import PartitionSpec as P

SUBSTEPS = 3
DT = 0.5
VISC = 0.4
F32 = jnp.float32
BF16 = jnp.bfloat16
MESH = pl.DeviceIdType.MESH


def kernel(
    dims,
    spec_hbm, mask_hbm, cour_hbm, inter_hbm, proj_hbm, cur_hbm, drag_hbm, cor_hbm,
    wave_hbm, curo_hbm,
    specx, adv, wmat, proj, maskv, cour, curv, dragv, corv,
    maskf, mask_b, fbuf, ystage, ysend, yrecv, yhalo,
    flow, stokes, vsend, vrecv, obuf, coutv,
    load_sem, hx_send, hx_recv, hy_send, hy_recv, av_send, av_recv,
    fx_send, fx_recv, fy_send, fy_recv, out_sem,
):
    nx, ny, nk, nl = dims
    gx, gy, core = lax.axis_index("gx"), lax.axis_index("gy"), lax.axis_index("comp")
    n_gx, n_gy = lax.axis_size("gx"), lax.axis_size("gy")
    west = (lax.rem(gx + n_gx - 1, n_gx), gy, core)
    east = (lax.rem(gx + 1, n_gx), gy, core)
    south = (gx, lax.rem(gy + n_gy - 1, n_gy), core)
    north = (gx, lax.rem(gy + 1, n_gy), core)
    other = 1 - core
    partner = (gx, gy, other)
    not_first = jnp.where(gy > 0, 1.0, 0.0).astype(F32)
    not_last = jnp.where(gy < n_gy - 1, 1.0, 0.0).astype(F32)

    def rows(start, count):
        return pl.ds(pl.multiple_of(start * ny, ny), count * ny)

    loads = []

    def load(src, dst):
        copy = pltpu.make_async_copy(src, dst, load_sem.at[len(loads)])
        copy.start()
        loads.append(copy)
        return copy

    spec_load = load(spec_hbm, specx.at[pl.ds(ny, nx * ny), :])
    mask_load = load(mask_hbm, maskv)
    cour_load = load(cour_hbm, cour)
    cur_load = load(cur_hbm, curv)
    own_k = pl.ds(pl.multiple_of(core * nk, nk), nk)
    oth_k = pl.ds(pl.multiple_of(other * nk, nk), nk)
    own_l = pl.ds(pl.multiple_of(core * nl, nl), nl)
    late = [
        load(drag_hbm, dragv),
        load(cor_hbm, corv),
        load(proj_hbm.at[0, own_l, own_k], proj.at[pl.ds(0, nl), pl.ds(0, nk)]),
        load(proj_hbm.at[0, own_l, oth_k], proj.at[pl.ds(0, nl), pl.ds(nk, nk)]),
        load(proj_hbm.at[1, own_l, own_k], proj.at[pl.ds(nl, nl), pl.ds(0, nk)]),
        load(proj_hbm.at[1, own_l, oth_k], proj.at[pl.ds(nl, nl), pl.ds(nk, nk)]),
        load(inter_hbm.at[own_k, own_k], wmat.at[pl.ds(0, nk), :]),
        load(inter_hbm.at[oth_k, own_k], wmat.at[pl.ds(nk, nk), :]),
    ]

    barrier = pltpu.get_barrier_semaphore()
    for peer in (west, east, south, north, partner):
        pl.semaphore_signal(barrier, inc=1, device_id=peer, device_id_type=MESH)

    def remote(src, dst, send, recv, peer):
        return pltpu.make_async_remote_copy(
            src_ref=src, dst_ref=dst, send_sem=send, recv_sem=recv,
            device_id=peer, device_id_type=MESH,
        )

    spec_load.wait()
    for x in range(nx):
        first = (1 + x) * ny
        ystage[0, x:x + 1, :] = specx[first:first + 16, :].astype(F32)[0:1]
        ystage[1, x:x + 1, :] = specx[first + ny - 16:first + ny, :].astype(F32)[15:16]
    ysend[...] = ystage[...].astype(BF16)

    pl.semaphore_wait(barrier, 5)
    hy = [
        remote(ysend.at[0], yrecv.at[1], hy_send.at[0], hy_recv.at[1], south),
        remote(ysend.at[1], yrecv.at[0], hy_send.at[1], hy_recv.at[0], north),
    ]
    hx = [
        remote(spec_hbm.at[rows(0, 1), :], specx.at[rows(nx + 1, 1), :], hx_send.at[0], hx_recv.at[1], west),
        remote(spec_hbm.at[rows(nx - 1, 1), :], specx.at[rows(0, 1), :], hx_send.at[1], hx_recv.at[0], east),
    ]
    for copy in hy + hx:
        copy.start()

    lane = lax.broadcasted_iota(jnp.int32, (nl, ny), 1)

    def pack(x, u, v, low, high):
        for c, q in ((0, u), (1, v)):
            spot = c * nx + x
            low = jnp.where(lane == spot, pltpu.roll(q, spot, 1), low)
            high = jnp.where(lane == spot, pltpu.roll(q, spot + 1, 1), high)
        return low, high

    def send_flow(s, low, high):
        vsend[s, 0] = low
        vsend[s, 1] = high
        copies = [
            remote(flow.at[s, 1], flow.at[s, nx + 1], fx_send.at[s, 0], fx_recv.at[s, 1], west),
            remote(flow.at[s, nx], flow.at[s, 0], fx_send.at[s, 1], fx_recv.at[s, 0], east),
            remote(vsend.at[s, 0], vrecv.at[s, 1], fy_send.at[s, 0], fy_recv.at[s, 1], south),
            remote(vsend.at[s, 1], vrecv.at[s, 0], fy_send.at[s, 1], fy_recv.at[s, 0], north),
        ]
        for copy in copies:
            copy.start()
        return copies

    zero = jnp.zeros((nl, ny), F32)
    cur_load.wait()

    def first_flow(x, carry):
        u = curv[pl.ds(x, nl, stride=nx), :]
        v = curv[pl.ds(nl * nx + x, nl, stride=nx), :]
        flow[0, x + 1, 0:nl, :] = u
        flow[0, x + 1, nl:2 * nl, :] = v
        return pack(x, u, v, *carry)

    sent = [send_flow(0, *lax.fori_loop(0, nx, first_flow, (zero, zero)))]

    mask_load.wait()
    cour_load.wait()
    own_mask = maskv[...].astype(F32)
    maskf[...] = own_mask
    turned = jnp.concatenate([own_mask, jnp.zeros((ny - nx, ny), F32)], axis=0).T
    for x in range(nx):
        mask_b[x * ny:(x + 1) * ny, :] = jnp.broadcast_to(turned[:, x:x + 1], (ny, 128))

    chunks = nk // 128
    for copy in hy:
        copy.wait_recv()
    for kc in range(chunks):
        ks = slice(kc * 128, (kc + 1) * 128)
        yhalo[0, kc] = yrecv[0, :, ks].astype(F32) * not_first
        yhalo[1, kc] = yrecv[1, :, ks].astype(F32) * not_last

    def advect(x, carry):
        mb = mask_b[rows(x, 1), :]
        for kc in range(chunks):
            ks = slice(kc * 128, (kc + 1) * 128)
            a, b = cour[0:1, ks], cour[1:2, ks]
            mag_a, mag_b = jnp.abs(a), jnp.abs(b)
            here = specx[rows(x + 1, 1), ks].astype(F32)
            fbuf[kc, 8:8 + ny, :] = here
            fbuf[kc, 7:8, :] = yhalo[0, kc, pl.ds(x, 1), :]
            fbuf[kc, 8 + ny:9 + ny, :] = yhalo[1, kc, pl.ds(x, 1), :]
            ux = jnp.where(a > 0, specx[rows(x, 1), ks].astype(F32), specx[rows(x + 2, 1), ks].astype(F32))
            uy = jnp.where(b > 0, fbuf[kc, 7:7 + ny, :], fbuf[kc, 9:9 + ny, :])
            new = (1.0 - mag_a - mag_b) * here + mag_a * ux + mag_b * uy
            adv[rows(x, 1), ks] = (mb * new).astype(BF16)
        swap(x).start()
        return carry

    def swap(x):
        return remote(
            adv.at[rows(x, 1), pl.ds(0, nk)], adv.at[rows(x, 1), pl.ds(nk, nk)],
            av_send.at[x], av_recv.at[x], partner,
        )

    lax.fori_loop(1, nx - 1, advect, 0)
    for copy in hx:
        copy.wait_recv()
    advect(0, 0)
    advect(nx - 1, 0)

    for copy in late:
        copy.wait()

    def drift(p, carry):
        swap(2 * p).wait_recv()
        swap(2 * p + 1).wait_recv()
        both = lax.dot_general(
            proj[...], adv[rows(2 * p, 2), :], (((1,), (1,)), ((), ())),
            preferred_element_type=F32,
        )
        stokes[2 * p] = both[:, :ny]
        stokes[2 * p + 1] = both[:, ny:]
        return carry

    lax.fori_loop(0, nx // 2, drift, 0)

    eye = lax.broadcasted_iota(jnp.int32, (nl, nl), 0) == lax.broadcasted_iota(jnp.int32, (nl, nl), 1)
    drag = jnp.sum(jnp.where(eye, jnp.broadcast_to(dragv[...], (nl, nl)), 0.0), axis=1, keepdims=True)
    drag = jnp.broadcast_to(drag, (nl, ny))
    cor = corv[...]

    def substep(s):
        for copy in sent[s]:
            copy.wait_recv()
        south_halo = vrecv[s, 0] * not_first
        north_halo = vrecv[s, 1] * not_last

        def sides(x, c, q):
            spot = c * nx + x
            low = jnp.where(lane == 0, pltpu.roll(south_halo, ny - spot, 1), pltpu.roll(q, 1, 1))
            high = jnp.where(lane == ny - 1, pltpu.roll(north_halo, ny - 1 - spot, 1), pltpu.roll(q, ny - 1, 1))
            return low, high

        def step(x, carry):
            lev_u, lev_v = pl.ds(0, nl), pl.ds(nl, nl)
            u, v = flow[s, x + 1, lev_u, :], flow[s, x + 1, lev_v, :]
            u_w, v_w = flow[s, x, lev_u, :], flow[s, x, lev_v, :]
            u_e, v_e = flow[s, x + 2, lev_u, :], flow[s, x + 2, lev_v, :]
            u_s, u_n = sides(x, 0, u)
            v_s, v_n = sides(x, 1, v)
            total = cor + 0.5 * (v_e - v_w) - 0.5 * (u_n - u_s)
            lap_u = u_e + u_w + u_n + u_s - 4.0 * u
            lap_v = v_e + v_w + v_n + v_s - 4.0 * v
            m = maskf[pl.ds(x, 1), :]
            u_new = m * (u + DT * (total * (v + stokes[x, lev_v, :]) - drag * u + VISC * lap_u))
            v_new = m * (v + DT * (-total * (u + stokes[x, lev_u, :]) - drag * v + VISC * lap_v))
            if s == SUBSTEPS - 1:
                coutv[pl.ds(x, nl, stride=nx), :] = u_new
                coutv[pl.ds(nl * nx + x, nl, stride=nx), :] = v_new
                return carry
            flow[s + 1, x + 1, lev_u, :] = u_new
            flow[s + 1, x + 1, lev_v, :] = v_new
            return pack(x, u_new, v_new, *carry)

        if s == SUBSTEPS - 1:
            lax.fori_loop(0, nx, step, 0)
        else:
            sent.append(send_flow(s + 1, *lax.fori_loop(0, nx, step, (zero, zero))))

    group, wide = 4, 256

    def put(g):
        return pltpu.make_async_copy(
            obuf.at[rows(g * group, group), :], wave_hbm.at[rows(g * group, group), :], out_sem.at[g]
        )

    def gain(g, carry):
        rs = rows(g * group, group)
        mb = mask_b[rs, :]
        mb = jnp.concatenate([mb] * (wide // 128), axis=1)
        for n in range(nk // wide):
            ns = slice(n * wide, (n + 1) * wide)
            got = jnp.dot(adv[rs, :], wmat[:, ns], preferred_element_type=F32)
            obuf[rs, ns] = (mb * (adv[rs, ns].astype(F32) + got)).astype(BF16)
        put(g).start()
        return carry

    groups = nx // group
    substep(0)
    lax.fori_loop(0, groups // 2, gain, 0)
    substep(1)
    lax.fori_loop(groups // 2, groups, gain, 0)
    substep(2)
    cout = pltpu.make_async_copy(coutv, curo_hbm, out_sem.at[groups])
    cout.start()

    for copy in hy + hx + [c for copies in sent for c in copies]:
        copy.wait_send()

    def drain(x, carry):
        swap(x).wait_send()
        return carry

    lax.fori_loop(0, nx, drain, 0)

    def drain_out(g, carry):
        put(g).wait()
        return carry

    lax.fori_loop(0, groups, drain_out, 0)
    cout.wait()


def local(spectrum, sea_mask, courant, interaction, stokes_proj, currents, level_drag):
    nx, ny, nk = spectrum.shape
    nl = currents.shape[1]
    ny_total = lax.axis_size("gy") * ny
    lat_index = lax.axis_index("gy") * ny + jnp.arange(ny)
    coriolis = jnp.sin(jnp.pi * ((lat_index.astype(F32) + 0.5) / ny_total - 0.5))[None, :]
    any_space = pl.BlockSpec(memory_space=pl.ANY)
    groups = nx // 4
    dma = pltpu.SemaphoreType.DMA
    wave, cur = pl.pallas_call(
        functools.partial(kernel, (nx, ny, nk, nl)),
        out_shape=(
            jax.ShapeDtypeStruct((nx * ny, nk), BF16),
            jax.ShapeDtypeStruct((2 * nl * nx, ny), F32),
        ),
        in_specs=[any_space] * 8,
        out_specs=(any_space, any_space),
        scratch_shapes=[
            pltpu.VMEM(((nx + 2) * ny, nk), BF16),
            pltpu.VMEM((nx * ny, 2 * nk), BF16),
            pltpu.VMEM((2 * nk, nk), BF16),
            pltpu.VMEM((2 * nl, 2 * nk), BF16),
            pltpu.VMEM((nx, ny), jnp.int32),
            pltpu.VMEM((2, nk), F32),
            pltpu.VMEM((2 * nl * nx, ny), F32),
            pltpu.VMEM((1, nl), F32),
            pltpu.VMEM((1, ny), F32),
            pltpu.VMEM((nx, ny), F32),
            pltpu.VMEM((nx * ny, 128), F32),
            pltpu.VMEM((nk // 128, ny + 16, 128), F32),
            pltpu.VMEM((2, nx, nk), F32),
            pltpu.VMEM((2, nx, nk), BF16),
            pltpu.VMEM((2, nx, nk), BF16),
            pltpu.VMEM((2, nk // 128, nx, 128), F32),
            pltpu.VMEM((SUBSTEPS, nx + 2, 2 * nl, ny), F32),
            pltpu.VMEM((nx, 2 * nl, ny), F32),
            pltpu.VMEM((SUBSTEPS, 2, nl, ny), F32),
            pltpu.VMEM((SUBSTEPS, 2, nl, ny), F32),
            pltpu.VMEM((nx * ny, nk), BF16),
            pltpu.VMEM((2 * nl * nx, ny), F32),
            dma((12,)),
            dma((2,)), dma((2,)), dma((2,)), dma((2,)),
            dma((nx,)), dma((nx,)),
            dma((SUBSTEPS, 2)), dma((SUBSTEPS, 2)), dma((SUBSTEPS, 2)), dma((SUBSTEPS, 2)),
            dma((groups + 1,)),
        ],
        compiler_params=pltpu.CompilerParams(
            collective_id=0, has_side_effects=True, vmem_limit_bytes=48 * 1024 * 1024
        ),
        name="wave_ocean",
    )(
        spectrum.reshape(nx * ny, nk),
        sea_mask,
        courant,
        interaction,
        jnp.transpose(stokes_proj, (0, 2, 1)),
        currents.reshape(2 * nl * nx, ny),
        level_drag[None, :],
        coriolis,
    )
    return wave.reshape(nx, ny, nk), cur.reshape(2, nl, nx, ny)


def solution(mesh):
    in_specs = (
        P("gx", "gy", "comp"),
        P("gx", "gy"),
        P(None, "comp"),
        P(),
        P(),
        P(None, "comp", "gx", "gy"),
        P("comp"),
    )
    out_specs = (P("gx", "gy", "comp"), P(None, "comp", "gx", "gy"))
    return jax.shard_map(local, mesh=mesh, in_specs=in_specs, out_specs=out_specs, check_vma=False)
```

time: 163 us -> 55.3 us (0.34)
  the two profiles are of different devices: /device:TPU:168 before, /device:TPU:1 now
where the time goes in v1:
time: 55.3 us; the launch traced here: 55 us
  Pallas kernels  46.6 us (84%)
  local copies, waits for them, and re-layouts  7.73 us (14%)
  between operations  0.66 us (1%)
    pallas_call x1, Pallas kernels, local(): pl.pallas_call(functools.partial(kernel, (nx, ny, nk, nl)), out_shape=(ja...  46.6 us
    unnamed x14, local copies, waits for them, and re-layouts  7.73 us

profile of v1, /device:TPU:1, one launch (start us, length us, event | category | flops | bytes accessed | tf_op | source)
XLA Modules:
  0.0 55.0 jit_solution(15655046491428754542)
XLA Ops:
  0.7 0.0 copy-start
  0.7 1.6 %copy-done = bf16[16,128,512]{2,1,0:T(8,128)(2,1)S(1)} copy-done((bf16[16,128,512]{2,1,0:T(8,128)(2,1)S(1)}, bf16[16,128,512]{2,1,0:T(8,128)(2,1)}, u32[]{:S(2)}) %copy-start) | copy-done | bytes 2097176
  2.3 0.0 copy-start.1
  2.3 1.0 %copy-done.1 = f32[2,32,16,128]{3,2,1,0:T(8,128)S(1)} copy-done((f32[2,32,16,128]{3,2,1,0:T(8,128)S(1)}, f32[2,32,16,128]{3,2,1,0:T(8,128)}, u32[]{:S(2)}) %copy-start.1) | copy-done | bytes 524312
  3.3 0.0 copy-start.2
  3.3 0.9 %copy-done.2 = bf16[2,1024,64]{1,2,0:T(8,128)(2,1)S(1)} copy-done((bf16[2,1024,64]{1,2,0:T(8,128)(2,1)S(1)}, bf16[2,1024,64]{1,2,0:T(8,128)(2,1)}, u32[]{:S(2)}) %copy-start.2) | copy-done | bytes 262168
  4.3 0.0 copy-start.3
  4.3 0.7 %copy-done.3 = s32[16,128]{1,0:T(8,128)S(1)} copy-done((s32[16,128]{1,0:T(8,128)S(1)}, s32[16,128]{1,0:T(8,128)}, u32[]{:S(2)}) %copy-start.3) | copy-done | bytes 8216
  5.0 0.0 copy-start.4
  5.0 0.7 %copy-done.4 = f32[2,512]{1,0:T(2,128)S(1)} copy-done((f32[2,512]{1,0:T(2,128)S(1)}, f32[2,512]{1,0:T(2,128)}, u32[]{:S(2)}) %copy-start.4) | copy-done | bytes 4120
  5.7 0.0 copy-start.5
  5.7 0.7 %copy-done.5 = f32[32]{0:T(128)S(1)} copy-done((f32[32]{0:T(128)S(1)}, f32[32]{0:T(128)}, u32[]{:S(2)}) %copy-start.5) | copy-done | bytes 152
  6.3 46.6 %wave_ocean.1 = (bf16[2048,512]{1,0:T(8,128)(2,1)S(1)}, f32[1024,128]{1,0:T(8,128)S(1)}) custom-call(bf16[2048,512]{1,0:T(8,128)(2,1)S(1)} %bitcast.6, s32[16,128]{1,0:T(8,128)S(1)} %copy-done.3, f32[2,512]{1,0:T(2,128)S(1)} %copy-done.4, bf16[1024,1024]{1,0:T(8,128)(2,1)} %inter_hbm.1, bf16[2,64,1024]{2,1,0:T(8,128)(2,1)S(1)} %bitcast.10, ...), custom_call_target="tpu_custom_call" | custom-call | tf_op jit(solution)/shard_map/wave_ocean/pallas_call | solution.py:289
  52.9 1.3 %copy.11 = bf16[16,128,512]{2,1,0:T(8,128)(2,1)} copy(bf16[16,128,512]{2,1,0:T(8,128)(2,1)S(1)} %bitcast.7) | data formatting | bytes 4194304
  54.2 0.8 %copy.12 = f32[2,32,16,128]{3,2,1,0:T(8,128)} copy(f32[2,32,16,128]{3,2,1,0:T(8,128)S(1)} %bitcast.9) | data formatting | bytes 1048576
  (1 shorter events, 0.0 us)
Async XLA Ops:
  0.7 1.6 %copy-start = (bf16[16,128,512]{2,1,0:T(8,128)(2,1)S(1)}, bf16[16,128,512]{2,1,0:T(8,128)(2,1)}, u32[]{:S(2)}) copy-start(bf16[16,128,512]{2,1,0:T(8,128)(2,1)} %param.7) | copy-start | bytes 6291460
  2.3 1.0 %copy-start.1 = (f32[2,32,16,128]{3,2,1,0:T(8,128)S(1)}, f32[2,32,16,128]{3,2,1,0:T(8,128)}, u32[]{:S(2)}) copy-start(f32[2,32,16,128]{3,2,1,0:T(8,128)} %param.12) | copy-start | bytes 1572868
  3.3 0.9 %copy-start.2 = (bf16[2,1024,64]{1,2,0:T(8,128)(2,1)S(1)}, bf16[2,1024,64]{1,2,0:T(8,128)(2,1)}, u32[]{:S(2)}) copy-start(bf16[2,1024,64]{1,2,0:T(8,128)(2,1)} %param.11) | copy-start | bytes 786436
  4.3 0.7 %copy-start.3 = (s32[16,128]{1,0:T(8,128)S(1)}, s32[16,128]{1,0:T(8,128)}, u32[]{:S(2)}) copy-start(s32[16,128]{1,0:T(8,128)} %mask_hbm.1) | copy-start | bytes 24580
  5.0 0.7 %copy-start.4 = (f32[2,512]{1,0:T(2,128)S(1)}, f32[2,512]{1,0:T(2,128)}, u32[]{:S(2)}) copy-start(f32[2,512]{1,0:T(2,128)} %cour_hbm.1) | copy-start | bytes 12292
  5.7 0.7 %copy-start.5 = (f32[32]{0:T(128)S(1)}, f32[32]{0:T(128)}, u32[]{:S(2)}) copy-start(f32[32]{0:T(128)} %param.13) | copy-start | bytes 388

commit v2 on v1

--- a/solution.py
+++ b/solution.py
@@ -20,7 +20,7 @@
     spec_hbm, mask_hbm, cour_hbm, inter_hbm, proj_hbm, cur_hbm, drag_hbm, cor_hbm,
     wave_hbm, curo_hbm,
     specx, adv, wmat, proj, maskv, cour, curv, dragv, corv,
-    maskf, mask_b, fbuf, ystage, ysend, yrecv, yhalo,
+    maskf, mask_b, drag_b, fbuf, ystage, ysend, yrecv, yhalo,
     flow, stokes, vsend, vrecv, obuf, coutv,
     load_sem, hx_send, hx_recv, hy_send, hy_recv, av_send, av_recv,
     fx_send, fx_recv, fy_send, fy_recv, out_sem,
@@ -76,26 +76,29 @@
             device_id=peer, device_id_type=MESH,
         )
 
+    pl.semaphore_wait(barrier, 5)
+    hx = [
+        remote(spec_hbm.at[rows(0, 1), :], specx.at[rows(nx + 1, 1), :], hx_send.at[0], hx_recv.at[1], west),
+        remote(spec_hbm.at[rows(nx - 1, 1), :], specx.at[rows(0, 1), :], hx_send.at[1], hx_recv.at[0], east),
+    ]
+    for copy in hx:
+        copy.start()
+
     spec_load.wait()
     for x in range(nx):
         first = (1 + x) * ny
         ystage[0, x:x + 1, :] = specx[first:first + 16, :].astype(F32)[0:1]
         ystage[1, x:x + 1, :] = specx[first + ny - 16:first + ny, :].astype(F32)[15:16]
     ysend[...] = ystage[...].astype(BF16)
-
-    pl.semaphore_wait(barrier, 5)
     hy = [
         remote(ysend.at[0], yrecv.at[1], hy_send.at[0], hy_recv.at[1], south),
         remote(ysend.at[1], yrecv.at[0], hy_send.at[1], hy_recv.at[0], north),
     ]
-    hx = [
-        remote(spec_hbm.at[rows(0, 1), :], specx.at[rows(nx + 1, 1), :], hx_send.at[0], hx_recv.at[1], west),
-        remote(spec_hbm.at[rows(nx - 1, 1), :], specx.at[rows(0, 1), :], hx_send.at[1], hx_recv.at[0], east),
-    ]
-    for copy in hy + hx:
+    for copy in hy:
         copy.start()
 
     lane = lax.broadcasted_iota(jnp.int32, (nl, ny), 1)
+    lev_u, lev_v = pl.ds(0, nl), pl.ds(nl, nl)
 
     def pack(x, u, v, low, high):
         for c, q in ((0, u), (1, v)):
@@ -104,18 +107,27 @@
             high = jnp.where(lane == spot, pltpu.roll(q, spot + 1, 1), high)
         return low, high
 
-    def send_flow(s, low, high):
-        vsend[s, 0] = low
-        vsend[s, 1] = high
-        copies = [
+    def flow_x(s):
+        return [
             remote(flow.at[s, 1], flow.at[s, nx + 1], fx_send.at[s, 0], fx_recv.at[s, 1], west),
             remote(flow.at[s, nx], flow.at[s, 0], fx_send.at[s, 1], fx_recv.at[s, 0], east),
+        ]
+
+    def flow_y(s):
+        return [
             remote(vsend.at[s, 0], vrecv.at[s, 1], fy_send.at[s, 0], fy_recv.at[s, 1], south),
             remote(vsend.at[s, 1], vrecv.at[s, 0], fy_send.at[s, 1], fy_recv.at[s, 0], north),
         ]
-        for copy in copies:
+
+    def send_x(s):
+        for copy in flow_x(s):
             copy.start()
-        return copies
+
+    def send_y(s, low, high):
+        vsend[s, 0] = low
+        vsend[s, 1] = high
+        for copy in flow_y(s):
+            copy.start()
 
     zero = jnp.zeros((nl, ny), F32)
     cur_load.wait()
@@ -123,11 +135,13 @@
     def first_flow(x, carry):
         u = curv[pl.ds(x, nl, stride=nx), :]
         v = curv[pl.ds(nl * nx + x, nl, stride=nx), :]
-        flow[0, x + 1, 0:nl, :] = u
-        flow[0, x + 1, nl:2 * nl, :] = v
+        flow[0, x + 1, lev_u, :] = u
+        flow[0, x + 1, lev_v, :] = v
         return pack(x, u, v, *carry)
 
-    sent = [send_flow(0, *lax.fori_loop(0, nx, first_flow, (zero, zero)))]
+    edges = lax.fori_loop(0, nx, first_flow, (zero, zero), unroll=4)
+    send_x(0)
+    send_y(0, *edges)
 
     mask_load.wait()
     cour_load.wait()
@@ -137,6 +151,12 @@
     for x in range(nx):
         mask_b[x * ny:(x + 1) * ny, :] = jnp.broadcast_to(turned[:, x:x + 1], (ny, 128))
 
+    for copy in late:
+        copy.wait()
+    eye = lax.broadcasted_iota(jnp.int32, (nl, nl), 0) == lax.broadcasted_iota(jnp.int32, (nl, nl), 1)
+    drag = jnp.sum(jnp.where(eye, jnp.broadcast_to(dragv[...], (nl, nl)), 0.0), axis=1, keepdims=True)
+    drag_b[...] = jnp.broadcast_to(drag, (nl, ny))
+
     chunks = nk // 128
     for copy in hy:
         copy.wait_recv()
@@ -144,6 +164,12 @@
         ks = slice(kc * 128, (kc + 1) * 128)
         yhalo[0, kc] = yrecv[0, :, ks].astype(F32) * not_first
         yhalo[1, kc] = yrecv[1, :, ks].astype(F32) * not_last
+
+    def swap(x):
+        return remote(
+            adv.at[rows(x, 1), pl.ds(0, nk)], adv.at[rows(x, 1), pl.ds(nk, nk)],
+            av_send.at[x], av_recv.at[x], partner,
+        )
 
     def advect(x, carry):
         mb = mask_b[rows(x, 1), :]
@@ -162,21 +188,6 @@
         swap(x).start()
         return carry
 
-    def swap(x):
-        return remote(
-            adv.at[rows(x, 1), pl.ds(0, nk)], adv.at[rows(x, 1), pl.ds(nk, nk)],
-            av_send.at[x], av_recv.at[x], partner,
-        )
-
-    lax.fori_loop(1, nx - 1, advect, 0)
-    for copy in hx:
-        copy.wait_recv()
-    advect(0, 0)
-    advect(nx - 1, 0)
-
-    for copy in late:
-        copy.wait()
-
     def drift(p, carry):
         swap(2 * p).wait_recv()
         swap(2 * p + 1).wait_recv()
@@ -188,80 +199,104 @@
         stokes[2 * p + 1] = both[:, ny:]
         return carry
 
-    lax.fori_loop(0, nx // 2, drift, 0)
-
-    eye = lax.broadcasted_iota(jnp.int32, (nl, nl), 0) == lax.broadcasted_iota(jnp.int32, (nl, nl), 1)
-    drag = jnp.sum(jnp.where(eye, jnp.broadcast_to(dragv[...], (nl, nl)), 0.0), axis=1, keepdims=True)
-    drag = jnp.broadcast_to(drag, (nl, ny))
-    cor = corv[...]
-
-    def substep(s):
-        for copy in sent[s]:
-            copy.wait_recv()
-        south_halo = vrecv[s, 0] * not_first
-        north_halo = vrecv[s, 1] * not_last
-
-        def sides(x, c, q):
+    def halo_y(s):
+        return vrecv[s, 0] * not_first, vrecv[s, 1] * not_last
+
+    def step(s, south_halo, north_halo, x, carry):
+        def sides(c, q):
             spot = c * nx + x
             low = jnp.where(lane == 0, pltpu.roll(south_halo, ny - spot, 1), pltpu.roll(q, 1, 1))
             high = jnp.where(lane == ny - 1, pltpu.roll(north_halo, ny - 1 - spot, 1), pltpu.roll(q, ny - 1, 1))
             return low, high
 
-        def step(x, carry):
-            lev_u, lev_v = pl.ds(0, nl), pl.ds(nl, nl)
-            u, v = flow[s, x + 1, lev_u, :], flow[s, x + 1, lev_v, :]
-            u_w, v_w = flow[s, x, lev_u, :], flow[s, x, lev_v, :]
-            u_e, v_e = flow[s, x + 2, lev_u, :], flow[s, x + 2, lev_v, :]
-            u_s, u_n = sides(x, 0, u)
-            v_s, v_n = sides(x, 1, v)
-            total = cor + 0.5 * (v_e - v_w) - 0.5 * (u_n - u_s)
-            lap_u = u_e + u_w + u_n + u_s - 4.0 * u
-            lap_v = v_e + v_w + v_n + v_s - 4.0 * v
-            m = maskf[pl.ds(x, 1), :]
-            u_new = m * (u + DT * (total * (v + stokes[x, lev_v, :]) - drag * u + VISC * lap_u))
-            v_new = m * (v + DT * (-total * (u + stokes[x, lev_u, :]) - drag * v + VISC * lap_v))
-            if s == SUBSTEPS - 1:
-                coutv[pl.ds(x, nl, stride=nx), :] = u_new
-                coutv[pl.ds(nl * nx + x, nl, stride=nx), :] = v_new
-                return carry
-            flow[s + 1, x + 1, lev_u, :] = u_new
-            flow[s + 1, x + 1, lev_v, :] = v_new
-            return pack(x, u_new, v_new, *carry)
-
+        u, v = flow[s, x + 1, lev_u, :], flow[s, x + 1, lev_v, :]
+        u_w, v_w = flow[s, x, lev_u, :], flow[s, x, lev_v, :]
+        u_e, v_e = flow[s, x + 2, lev_u, :], flow[s, x + 2, lev_v, :]
+        u_s, u_n = sides(0, u)
+        v_s, v_n = sides(1, v)
+        drag = drag_b[...]
+        total = corv[...] + 0.5 * (v_e - v_w) - 0.5 * (u_n - u_s)
+        lap_u = u_e + u_w + u_n + u_s - 4.0 * u
+        lap_v = v_e + v_w + v_n + v_s - 4.0 * v
+        m = maskf[pl.ds(x, 1), :]
+        u_new = m * (u + DT * (total * (v + stokes[x, lev_v, :]) - drag * u + VISC * lap_u))
+        v_new = m * (v + DT * (-total * (u + stokes[x, lev_u, :]) - drag * v + VISC * lap_v))
         if s == SUBSTEPS - 1:
-            lax.fori_loop(0, nx, step, 0)
-        else:
-            sent.append(send_flow(s + 1, *lax.fori_loop(0, nx, step, (zero, zero))))
-
-    group, wide = 4, 256
-
-    def put(g):
+            coutv[pl.ds(x, nl, stride=nx), :] = u_new
+            coutv[pl.ds(nl * nx + x, nl, stride=nx), :] = v_new
+            return carry
+        flow[s + 1, x + 1, lev_u, :] = u_new
+        flow[s + 1, x + 1, lev_v, :] = v_new
+        return pack(x, u_new, v_new, *carry)
+
+    wide = 256
+
+    def put(x):
         return pltpu.make_async_copy(
-            obuf.at[rows(g * group, group), :], wave_hbm.at[rows(g * group, group), :], out_sem.at[g]
+            obuf.at[rows(x, 2), :], wave_hbm.at[rows(x, 2), :], out_sem.at[x // 2]
         )
 
-    def gain(g, carry):
-        rs = rows(g * group, group)
+    def gain(x, count):
+        rs = rows(x, count)
         mb = mask_b[rs, :]
         mb = jnp.concatenate([mb] * (wide // 128), axis=1)
         for n in range(nk // wide):
             ns = slice(n * wide, (n + 1) * wide)
             got = jnp.dot(adv[rs, :], wmat[:, ns], preferred_element_type=F32)
             obuf[rs, ns] = (mb * (adv[rs, ns].astype(F32) + got)).astype(BF16)
-        put(g).start()
-        return carry
-
-    groups = nx // group
-    substep(0)
-    lax.fori_loop(0, groups // 2, gain, 0)
-    substep(1)
-    lax.fori_loop(groups // 2, groups, gain, 0)
-    substep(2)
-    cout = pltpu.make_async_copy(coutv, curo_hbm, out_sem.at[groups])
+        for part in range(0, count, 2):
+            put(x + part).start()
+
+    def arrived(copies):
+        for copy in copies:
+            copy.wait_recv()
+
+    lax.fori_loop(1, nx - 1, advect, 0)
+    lax.fori_loop(1, nx // 2 - 1, drift, 0)
+    arrived(flow_y(0))
+    halo = halo_y(0)
+    edges = lax.fori_loop(2, nx - 2, functools.partial(step, 0, *halo), (zero, zero), unroll=2)
+    for x in range(4, nx - 4, 4):
+        gain(x, 4)
+
+    for copy in hx:
+        copy.wait_recv()
+    advect(0, 0)
+    advect(nx - 1, 0)
+    arrived(flow_x(0))
+    gain(2, 2)
+    drift(0, 0)
+    drift(nx // 2 - 1, 0)
+    for x in (0, nx - 1):
+        edges = step(0, *halo, x, edges)
+    send_x(1)
+    for x in (1, nx - 2):
+        edges = step(0, *halo, x, edges)
+    send_y(1, *edges)
+
+    gain(nx - 4, 4)
+    arrived(flow_x(1))
+    arrived(flow_y(1))
+    halo = halo_y(1)
+    edges = (zero, zero)
+    for x in (0, nx - 1):
+        edges = step(1, *halo, x, edges)
+    send_x(2)
+    edges = lax.fori_loop(1, nx - 1, functools.partial(step, 1, *halo), edges, unroll=2)
+    send_y(2, *edges)
+
+    gain(0, 2)
+    arrived(flow_x(2))
+    arrived(flow_y(2))
+    lax.fori_loop(0, nx, functools.partial(step, 2, *halo_y(2)), 0, unroll=2)
+    cout = pltpu.make_async_copy(coutv, curo_hbm, out_sem.at[nx // 2])
     cout.start()
 
-    for copy in hy + hx + [c for copies in sent for c in copies]:
+    for copy in hy + hx:
         copy.wait_send()
+    for s in range(SUBSTEPS):
+        for copy in flow_x(s) + flow_y(s):
+            copy.wait_send()
 
     def drain(x, carry):
         swap(x).wait_send()
@@ -270,10 +305,10 @@
     lax.fori_loop(0, nx, drain, 0)
 
     def drain_out(g, carry):
-        put(g).wait()
+        put(2 * g).wait()
         return carry
 
-    lax.fori_loop(0, groups, drain_out, 0)
+    lax.fori_loop(0, nx // 2, drain_out, 0)
     cout.wait()
 
 
@@ -284,7 +319,6 @@
     lat_index = lax.axis_index("gy") * ny + jnp.arange(ny)
     coriolis = jnp.sin(jnp.pi * ((lat_index.astype(F32) + 0.5) / ny_total - 0.5))[None, :]
     any_space = pl.BlockSpec(memory_space=pl.ANY)
-    groups = nx // 4
     dma = pltpu.SemaphoreType.DMA
     wave, cur = pl.pallas_call(
         functools.partial(kernel, (nx, ny, nk, nl)),
@@ -306,6 +340,7 @@
             pltpu.VMEM((1, ny), F32),
             pltpu.VMEM((nx, ny), F32),
             pltpu.VMEM((nx * ny, 128), F32),
+            pltpu.VMEM((nl, ny), F32),
             pltpu.VMEM((nk // 128, ny + 16, 128), F32),
             pltpu.VMEM((2, nx, nk), F32),
             pltpu.VMEM((2, nx, nk), BF16),
@@ -321,10 +356,10 @@
             dma((2,)), dma((2,)), dma((2,)), dma((2,)),
             dma((nx,)), dma((nx,)),
             dma((SUBSTEPS, 2)), dma((SUBSTEPS, 2)), dma((SUBSTEPS, 2)), dma((SUBSTEPS, 2)),
-            dma((groups + 1,)),
+            dma((nx // 2 + 1,)),
         ],
         compiler_params=pltpu.CompilerParams(
-            collective_id=0, has_side_effects=True, vmem_limit_bytes=48 * 1024 * 1024
+            collective_id=0, has_side_effects=True, vmem_limit_bytes=67_000_000
         ),
         name="wave_ocean",
     )(

time: 55.3 us -> 52.9 us (0.957)
  local copies, waits for them, and re-layouts: 7.73 us -> 3.95 us
  Pallas kernels: 46.6 us -> 47.6 us
    unnamed x14 -> x4, local copies, waits for them, and re-layouts: 7.73 us -> 3.95 us
    pallas_call x1, Pallas kernels: 46.6 us -> 47.6 us  [local(): pl.pallas_call(functools.partial(kernel, (nx, ny, nk, nl)), out_shape=(ja...]
where the time goes in v2:
time: 52.9 us; the launch traced here: 52.7 us
  Pallas kernels  47.6 us (90%)
  local copies, waits for them, and re-layouts  3.95 us (7%)
  between operations  0.65 us (1%)
  other arithmetic  0.56 us (1%)
    pallas_call x1, Pallas kernels, local(): pl.pallas_call(functools.partial(kernel, (nx, ny, nk, nl)), out_shape=(ja...  47.6 us
    unnamed x4, local copies, waits for them, and re-layouts  3.95 us

profile of v2, /device:TPU:1, one launch (start us, length us, event | category | flops | bytes accessed | tf_op | source)
XLA Modules:
  0.0 52.7 jit_solution(6384260042939773513)
XLA Ops:
  0.6 0.6 %multiply_sine_fusion.cor_hbm = f32[1,128]{1,0:T(1,128)} fusion(s32[]{:T(128)S(6)} %mul.16), kind=kLoop, calls=%fused_computation | loop fusion | flops 768 | bytes 516 | tf_op jit(solution)/shard_map/sin | solution.py:320
  1.2 47.6 %wave_ocean.1 = (bf16[2048,512]{1,0:T(8,128)(2,1)}, f32[1024,128]{1,0:T(8,128)}) custom-call(bf16[2048,512]{1,0:T(8,128)(2,1)} %bitcast.6, s32[16,128]{1,0:T(8,128)} %mask_hbm.1, f32[2,512]{1,0:T(2,128)} %cour_hbm.1, bf16[1024,1024]{1,0:T(8,128)(2,1)} %inter_hbm.1, bf16[2,64,1024]{2,1,0:T(8,128)(2,1)} %bitcast.10, f32[1024,128]{1,0:T(8,128)} %bitcast.8, ...), custom_call_target="tpu_custom_call" | custom-call | tf_op jit(solution)/shard_map/wave_ocean/pallas_call | solution.py:323
  48.8 0.0 copy-start
  48.8 3.2 %copy.11 = bf16[16,128,512]{2,1,0:T(8,128)(2,1)} copy(bf16[16,128,512]{2,1,0:T(8,128)(2,1)} %bitcast.7) | data formatting | bytes 4194304
  51.9 0.0 copy-done
  51.9 0.8 %copy.12 = f32[2,32,16,128]{3,2,1,0:T(8,128)} copy(f32[2,32,16,128]{3,2,1,0:T(8,128)S(1)} %bitcast.9) | data formatting | bytes 1048576
Async XLA Ops:
  48.8 3.2 %copy-start = (f32[1024,128]{1,0:T(8,128)S(1)}, f32[1024,128]{1,0:T(8,128)}, u32[]{:S(2)}) copy-start(f32[1024,128]{1,0:T(8,128)} %get-tuple-element.5) | copy-start | bytes 1572868

commit v3 on v2

v3 whole, which is shorter than its diff:
```python
import functools

import jax
import jax.numpy as jnp
from jax import lax
from jax.experimental import pallas as pl
from jax.experimental.pallas import tpu as pltpu
from jax.sharding import PartitionSpec as P

SUBSTEPS = 3
DT = 0.5
VISC = 0.4
F32 = jnp.float32
BF16 = jnp.bfloat16
MESH = pl.DeviceIdType.MESH


PAD = 8
LANES = 128


def advance(flow, stokes, mask_t, cor_t, drag, ny, i, store):
    block = 32
    for first in range(0, ny, block):
        at = PAD + first
        u, v = (flow[c, i + 1, at:at + block, :] for c in (0, 1))
        u_w, v_w = (flow[c, i, at:at + block, :] for c in (0, 1))
        u_e, v_e = (flow[c, i + 2, at:at + block, :] for c in (0, 1))
        u_s, v_s = (flow[c, i + 1, at - 1:at + block - 1, :] for c in (0, 1))
        u_n, v_n = (flow[c, i + 1, at + 1:at + block + 1, :] for c in (0, 1))
        rs = pl.ds(pl.multiple_of(i * ny + first, block), block)
        total = cor_t[first:first + block, :] + 0.5 * (v_e - v_w) - 0.5 * (u_n - u_s)
        lap_u = u_e + u_w + u_n + u_s - 4.0 * u
        lap_v = v_e + v_w + v_n + v_s - 4.0 * v
        m = mask_t[rs, :]
        u_new = m * (u + DT * (total * (v + stokes[rs, LANES:2 * LANES]) - drag * u + VISC * lap_u))
        v_new = m * (v + DT * (-total * (u + stokes[rs, 0:LANES]) - drag * v + VISC * lap_v))
        store(i, first, block, u_new, v_new)


def kernel(
    dims,
    spec_hbm, mask_hbm, cour_hbm, inter_hbm, proj_hbm, cur_hbm, drag_hbm,
    wave, last, stokes, mask_t, cor_t, drag_t,
    specx, adv, wmat, proj, projp, maskv, cour, curv, dragv,
    mask_b, fbuf, ystage, ysend, yrecv, yhalo,
    flow, xsend, xrecv, vsend, vrecv,
    load_sem, hx_send, hx_recv, hy_send, hy_recv, av_send, av_recv,
    fx_send, fx_recv, fy_send, fy_recv,
):
    nx, ny, nk, nl = dims
    groups = LANES // nl
    tiles = nx // groups
    gx, gy, core = lax.axis_index("gx"), lax.axis_index("gy"), lax.axis_index("comp")
    n_gx, n_gy = lax.axis_size("gx"), lax.axis_size("gy")
    west = (lax.rem(gx + n_gx - 1, n_gx), gy, core)
    east = (lax.rem(gx + 1, n_gx), gy, core)
    south = (gx, lax.rem(gy + n_gy - 1, n_gy), core)
    north = (gx, lax.rem(gy + 1, n_gy), core)
    other = 1 - core
    partner = (gx, gy, other)
    not_first = jnp.where(gy > 0, 1.0, 0.0).astype(F32)
    not_last = jnp.where(gy < n_gy - 1, 1.0, 0.0).astype(F32)
    scope = jax.named_scope

    def rows(start, count):
        return pl.ds(pl.multiple_of(start * ny, ny), count * ny)

    barrier = pltpu.get_barrier_semaphore()
    for peer in (west, east, south, north, partner):
        pl.semaphore_signal(barrier, inc=1, device_id=peer, device_id_type=MESH)

    loads = []

    def load(src, dst):
        copy = pltpu.make_async_copy(src, dst, load_sem.at[len(loads)])
        copy.start()
        loads.append(copy)
        return copy

    spec_load = load(spec_hbm, specx.at[pl.ds(ny, nx * ny), :])
    cur_load = load(cur_hbm, curv)
    mask_load = load(mask_hbm, maskv)
    cour_load = load(cour_hbm, cour)
    own_k = pl.ds(pl.multiple_of(core * nk, nk), nk)
    oth_k = pl.ds(pl.multiple_of(other * nk, nk), nk)
    own_l = pl.ds(pl.multiple_of(core * nl, nl), nl)
    proj_load = [
        load(proj_hbm.at[c, own_l, ks], proj.at[pl.ds(c * nl, nl), pl.ds(half * nk, nk)])
        for c in (0, 1) for half, ks in ((0, own_k), (1, oth_k))
    ]
    drag_load = load(drag_hbm, dragv)
    w_load = [
        load(inter_hbm.at[own_k, own_k], wmat.at[pl.ds(0, nk), :]),
        load(inter_hbm.at[oth_k, own_k], wmat.at[pl.ds(nk, nk), :]),
    ]

    def remote(src, dst, send, recv, peer):
        return pltpu.make_async_remote_copy(
            src_ref=src, dst_ref=dst, send_sem=send, recv_sem=recv,
            device_id=peer, device_id_type=MESH,
        )

    with scope("t_barrier"):
        pl.semaphore_wait(barrier, 5)
    hx = [
        remote(spec_hbm.at[rows(0, 1), :], specx.at[rows(nx + 1, 1), :], hx_send.at[0], hx_recv.at[1], west),
        remote(spec_hbm.at[rows(nx - 1, 1), :], specx.at[rows(0, 1), :], hx_send.at[1], hx_recv.at[0], east),
    ]
    for copy in hx:
        copy.start()

    with scope("t_spec"):
        spec_load.wait()
    for x in range(nx):
        first = (1 + x) * ny
        ystage[0, x:x + 1, :] = specx[first:first + 16, :].astype(F32)[0:1]
        ystage[1, x:x + 1, :] = specx[first + ny - 16:first + ny, :].astype(F32)[15:16]
    ysend[...] = ystage[...].astype(BF16)
    hy = [
        remote(ysend.at[0], yrecv.at[1], hy_send.at[0], hy_recv.at[1], south),
        remote(ysend.at[1], yrecv.at[0], hy_send.at[1], hy_recv.at[0], north),
    ]
    for copy in hy:
        copy.start()

    inner = slice(PAD, PAD + ny)
    lane = lax.broadcasted_iota(jnp.int32, (ny, LANES), 1)
    half_lane = lax.broadcasted_iota(jnp.int32, (ny // 2, LANES), 1)
    half = ny // 2

    def state(s):
        return last if s == SUBSTEPS - 1 else flow.at[s]

    def flow_x(s):
        return [
            remote(xsend.at[s, 0], xrecv.at[s, 1], fx_send.at[s, 0], fx_recv.at[s, 1], west),
            remote(xsend.at[s, 1], xrecv.at[s, 0], fx_send.at[s, 1], fx_recv.at[s, 0], east),
        ]

    def flow_y(s):
        return [
            remote(vsend.at[s, 0], vrecv.at[s, 1], fy_send.at[s, 0], fy_recv.at[s, 1], south),
            remote(vsend.at[s, 1], vrecv.at[s, 0], fy_send.at[s, 1], fy_recv.at[s, 0], north),
        ]

    def turn(q, lanes):
        return pltpu.roll(q, lanes % LANES, 1) if lanes % LANES else q

    def send_flow(s):
        now = state(s)
        for side, tile, group in ((0, 1, 0), (1, tiles, groups - 1)):
            packed = None
            for c in (0, 1):
                for h in (0, 1):
                    g = 2 * c + h
                    part = turn(now[c, tile, PAD + h * half:PAD + (h + 1) * half, :], nl * (g - group))
                    packed = part if packed is None else jnp.where(half_lane >= nl * g, part, packed)
            xsend[s, side] = packed
        for copy in flow_x(s):
            copy.start()
        for c in (0, 1):
            for i in range(tiles):
                r = c * tiles + i
                vsend[s, 0, r:r + 1, :] = now[c, i + 1, PAD:PAD + 1, :]
                vsend[s, 1, r:r + 1, :] = now[c, i + 1, PAD + ny - 1:PAD + ny, :]
        for copy in flow_y(s):
            copy.start()

    def take_flow(s):
        now = state(s)
        for copy in flow_x(s):
            copy.wait_recv()
        for c in (0, 1):
            for h in (0, 1):
                g = 2 * c + h
                rs = slice(PAD + h * half, PAD + (h + 1) * half)
                from_west = turn(xrecv[s, 0], -nl * g)
                from_east = turn(xrecv[s, 1], nl * (groups - 1 - g))
                now[c, 0, rs, :] = jnp.where(half_lane < nl, from_west, turn(now[c, tiles, rs, :], nl))
                now[c, tiles + 1, rs, :] = jnp.where(
                    half_lane >= LANES - nl, from_east, turn(now[c, 1, rs, :], -nl)
                )
        for copy in flow_y(s):
            copy.wait_recv()
        for c in (0, 1):
            for i in range(tiles):
                r = c * tiles + i
                now[c, i + 1, PAD - 1:PAD, :] = vrecv[s, 0, r:r + 1, :] * not_first
                now[c, i + 1, PAD + ny:PAD + ny + 1, :] = vrecv[s, 1, r:r + 1, :] * not_last

    with scope("t_cur"):
        cur_load.wait()
    for c in (0, 1):
        for i in range(tiles):
            tile = jnp.concatenate(
                [curv[pl.ds(c * nl * nx + q * tiles + i, nl, stride=nx), :] for q in range(groups)], axis=0
            )
            flow[0, c, i + 1, inner, :] = tile.T
    send_flow(0)

    mask_load.wait()
    cour_load.wait()
    turned = jnp.concatenate([maskv[...].astype(F32), jnp.zeros((ny - nx, ny), F32)], axis=0).T
    for x in range(nx):
        mask_b[x * ny:(x + 1) * ny, :] = jnp.broadcast_to(turned[:, x:x + 1], (ny, LANES))
    for i in range(tiles):
        mixed = mask_b[i * ny:(i + 1) * ny, :]
        for q in range(1, groups):
            x = q * tiles + i
            mixed = jnp.where(lane >= nl * q, mask_b[x * ny:(x + 1) * ny, :], mixed)
        mask_t[i * ny:(i + 1) * ny, :] = mixed

    lat = (gy * ny + lax.broadcasted_iota(jnp.int32, (ny, LANES), 0)).astype(F32)
    cor_t[...] = jnp.sin(jnp.pi * ((lat + 0.5) / (n_gy * ny) - 0.5))

    with scope("t_late"):
        for copy in proj_load:
            copy.wait()
        drag_load.wait()
        for copy in w_load:
            copy.wait()
    drag = dragv[...]
    drag_t[...] = jnp.broadcast_to(jnp.concatenate([drag] * groups, axis=1), drag_t.shape)
    for q in range(groups):
        projp[q] = jnp.zeros(projp.shape[1:], BF16)
        for c in (0, 1):
            projp[q, c * LANES + q * nl:c * LANES + (q + 1) * nl, :] = proj[c * nl:(c + 1) * nl, :]

    chunks = nk // 128
    with scope("t_hy"):
        for copy in hy:
            copy.wait_recv()
    for kc in range(chunks):
        ks = slice(kc * 128, (kc + 1) * 128)
        yhalo[0, kc] = yrecv[0, :, ks].astype(F32) * not_first
        yhalo[1, kc] = yrecv[1, :, ks].astype(F32) * not_last

    def swap(x):
        return remote(
            adv.at[rows(x, 1), pl.ds(0, nk)], adv.at[rows(x, 1), pl.ds(nk, nk)],
            av_send.at[x], av_recv.at[x], partner,
        )

    def advect(x, carry):
        mb = mask_b[rows(x, 1), :]
        for kc in range(chunks):
            ks = slice(kc * 128, (kc + 1) * 128)
            a, b = cour[0:1, ks], cour[1:2, ks]
            mag_a, mag_b = jnp.abs(a), jnp.abs(b)
            here = specx[rows(x + 1, 1), ks].astype(F32)
            fbuf[kc, 8:8 + ny, :] = here
            fbuf[kc, 7:8, :] = yhalo[0, kc, pl.ds(x, 1), :]
            fbuf[kc, 8 + ny:9 + ny, :] = yhalo[1, kc, pl.ds(x, 1), :]
            ux = jnp.where(a > 0, specx[rows(x, 1), ks].astype(F32), specx[rows(x + 2, 1), ks].astype(F32))
            uy = jnp.where(b > 0, fbuf[kc, 7:7 + ny, :], fbuf[kc, 9:9 + ny, :])
            new = (1.0 - mag_a - mag_b) * here + mag_a * ux + mag_b * uy
            adv[rows(x, 1), ks] = (mb * new).astype(BF16)
        swap(x).start()
        return carry

    def drift(q, fresh):
        for x in range(q * tiles, (q + 1) * tiles):
            swap(x).wait_recv()
        part = lax.dot_general(
            adv[rows(q * tiles, tiles), :], projp[q], (((1,), (1,)), ((), ())),
            preferred_element_type=F32,
        )
        stokes[...] = part if fresh else stokes[...] + part

    drag_row = drag_t[0:1, :]

    def substep(s):
        now, then = state(s), state(s + 1)

        def store(i, first, block, u_new, v_new):
            at = slice(PAD + first, PAD + first + block)
            then[0, i + 1, at, :] = u_new
            then[1, i + 1, at, :] = v_new

        def one(i, carry):
            advance(now, stokes, mask_t, cor_t, drag_row, ny, i, store)
            return carry

        lax.fori_loop(0, tiles, one, 0)

    wide = 256

    def gain(p, carry):
        rs = rows(p * 4, 4)
        mb = mask_b[rs, :]
        mb = jnp.concatenate([mb] * (wide // 128), axis=1)
        for n in range(nk // wide):
            ns = slice(n * wide, (n + 1) * wide)
            got = jnp.dot(adv[rs, :], wmat[:, ns], preferred_element_type=F32)
            wave[rs, ns] = (mb * (adv[rs, ns].astype(F32) + got)).astype(BF16)
        return carry

    with scope("t_advect"):
        lax.fori_loop(1, nx - 1, advect, 0)
    with scope("t_hx"):
        for copy in hx:
            copy.wait_recv()
    with scope("t_edge"):
        for x in (0, nx - 1):
            advect(x, 0)
    with scope("t_drift"):
        for n, q in enumerate(list(range(1, groups - 1)) + [0, groups - 1]):
            drift(q, n == 0)
    with scope("t_take0"):
        take_flow(0)
    with scope("t_sub0"):
        substep(0)
        send_flow(1)
    with scope("t_gainA"):
        lax.fori_loop(0, nx // 4 - 1, gain, 0)
    with scope("t_take1"):
        take_flow(1)
    with scope("t_sub1"):
        substep(1)
        send_flow(2)
    with scope("t_gainB"):
        gain(nx // 4 - 1, 0)
    with scope("t_take2"):
        take_flow(2)

    with scope("t_out"):
        for copy in hy + hx:
            copy.wait_send()
        for s in range(SUBSTEPS):
            for copy in flow_x(s) + flow_y(s):
                copy.wait_send()

        def drain(x, carry):
            swap(x).wait_send()
            return carry

        lax.fori_loop(0, nx, drain, 0)


def finish(
    dims,
    wave, last, stokes, mask_t, cor_t, drag_t,
    wave_hbm, curo_hbm,
    done, coutv, out_sem,
):
    nx, ny, nk, nl = dims
    groups = LANES // nl
    tiles = nx // groups
    put = pltpu.make_async_copy(wave, wave_hbm, out_sem.at[0])
    put.start()
    drag_row = drag_t[0:1, :]

    def store(i, first, block, u_new, v_new):
        done[0, i, first:first + block, :] = u_new
        done[1, i, first:first + block, :] = v_new

    puts = [put]
    for i in range(tiles):
        advance(last, stokes, mask_t, cor_t, drag_row, ny, i, store)
    for c in (0, 1):
        for i in range(tiles):
            tile = done[c, i].T
            for q in range(groups):
                coutv[pl.ds(c * nl * nx + q * tiles + i, nl, stride=nx), :] = tile[q * nl:(q + 1) * nl]
        part = pl.ds(c * nl * nx, nl * nx)
        put = pltpu.make_async_copy(coutv.at[part, :], curo_hbm.at[part, :], out_sem.at[1 + c])
        put.start()
        puts.append(put)
    for put in puts:
        put.wait()


def local(spectrum, sea_mask, courant, interaction, stokes_proj, currents, level_drag):
    nx, ny, nk = spectrum.shape
    nl = currents.shape[1]
    groups = LANES // nl
    tiles = nx // groups
    dims = (nx, ny, nk, nl)
    hbm = pl.BlockSpec(memory_space=pltpu.HBM)
    vmem = pl.BlockSpec(memory_space=pltpu.VMEM)
    dma = pltpu.SemaphoreType.DMA
    between = pl.pallas_call(
        functools.partial(kernel, dims),
        out_shape=(
            jax.ShapeDtypeStruct((nx * ny, nk), BF16),
            jax.ShapeDtypeStruct((2, tiles + 2, ny + 2 * PAD, LANES), F32),
            jax.ShapeDtypeStruct((tiles * ny, 2 * LANES), F32),
            jax.ShapeDtypeStruct((tiles * ny, LANES), F32),
            jax.ShapeDtypeStruct((ny, LANES), F32),
            jax.ShapeDtypeStruct((8, LANES), F32),
        ),
        in_specs=[hbm] * 7,
        out_specs=(vmem,) * 6,
        scratch_shapes=[
            pltpu.VMEM(((nx + 2) * ny, nk), BF16),
            pltpu.VMEM((nx * ny, 2 * nk), BF16),
            pltpu.VMEM((2 * nk, nk), BF16),
            pltpu.VMEM((2 * nl, 2 * nk), BF16),
            pltpu.VMEM((groups, 2 * LANES, 2 * nk), BF16),
            pltpu.VMEM((nx, ny), jnp.int32),
            pltpu.VMEM((2, nk), F32),
            pltpu.VMEM((2 * nl * nx, ny), F32),
            pltpu.VMEM((1, nl), F32),
            pltpu.VMEM((nx * ny, 128), F32),
            pltpu.VMEM((nk // 128, ny + 16, 128), F32),
            pltpu.VMEM((2, nx, nk), F32),
            pltpu.VMEM((2, nx, nk), BF16),
            pltpu.VMEM((2, nx, nk), BF16),
            pltpu.VMEM((2, nk // 128, nx, 128), F32),
            pltpu.VMEM((SUBSTEPS - 1, 2, tiles + 2, ny + 2 * PAD, LANES), F32),
            pltpu.VMEM((SUBSTEPS, 2, ny // 2, LANES), F32),
            pltpu.VMEM((SUBSTEPS, 2, ny // 2, LANES), F32),
            pltpu.VMEM((SUBSTEPS, 2, 2 * tiles, LANES), F32),
            pltpu.VMEM((SUBSTEPS, 2, 2 * tiles, LANES), F32),
            dma((12,)),
            dma((2,)), dma((2,)), dma((2,)), dma((2,)),
            dma((nx,)), dma((nx,)),
            dma((SUBSTEPS, 2)), dma((SUBSTEPS, 2)), dma((SUBSTEPS, 2)), dma((SUBSTEPS, 2)),
        ],
        compiler_params=pltpu.CompilerParams(
            collective_id=0, has_side_effects=True, vmem_limit_bytes=40 * 1024 * 1024
        ),
        name="wave_ocean",
    )(*(pltpu.with_memory_space_constraint(each, pltpu.HBM) for each in (
        spectrum.reshape(nx * ny, nk),
        sea_mask,
        courant,
        interaction,
        jnp.transpose(stokes_proj, (0, 2, 1)),
        currents.reshape(2 * nl * nx, ny),
        level_drag[None, :],
    )))
    wave, cur = pl.pallas_call(
        functools.partial(finish, dims),
        out_shape=(
            jax.ShapeDtypeStruct((nx * ny, nk), BF16),
            jax.ShapeDtypeStruct((2 * nl * nx, ny), F32),
        ),
        in_specs=[vmem] * 6,
        out_specs=(hbm, hbm),
        scratch_shapes=[
            pltpu.VMEM((2, tiles, ny, LANES), F32),
            pltpu.VMEM((2 * nl * nx, ny), F32),
            dma((3,)),
        ],
        compiler_params=pltpu.CompilerParams(vmem_limit_bytes=40 * 1024 * 1024),
        name="last_substep",
    )(*between)
    return wave.reshape(nx, ny, nk), cur.reshape(2, nl, nx, ny)


def solution(mesh):
    in_specs = (
        P("gx", "gy", "comp"),
        P("gx", "gy"),
        P(None, "comp"),
        P(),
        P(),
        P(None, "comp", "gx", "gy"),
        P("comp"),
    )
    out_specs = (P("gx", "gy", "comp"), P(None, "comp", "gx", "gy"))
    return jax.shard_map(local, mesh=mesh, in_specs=in_specs, out_specs=out_specs, check_vma=False)
```

time: 52.9 us -> 44.1 us (0.83)
  Pallas kernels: 47.6 us -> 43.4 us
  local copies, waits for them, and re-layouts: 3.95 us -> 0 us
  other arithmetic: 0.56 us -> 0 us
    pallas_call x1 -> x2, Pallas kernels: 47.6 us -> 43.4 us  [the longest x1 41.6 us: local(): pl.pallas_call(functools.partial(kernel, dims), out_shape=(jax.ShapeDtype...]
    unnamed x4 -> x0, local copies, waits for them, and re-layouts: 3.95 us -> none
    sin x1 -> x0, other arithmetic: 0.56 us -> none  [local(): jnp.sin(jnp.pi * ((lat_index.astype(F32) + 0.5) / ny_total - 0.5))[None, :]]
where the time goes in v3:
time: 44.1 us; the launch traced here: 44 us
  Pallas kernels  43.4 us (98%)
  between operations  0.64 us (1%)
    pallas_call x1, Pallas kernels, local(): pl.pallas_call(functools.partial(kernel, dims), out_shape=(jax.ShapeDtype...  41.6 us
    pallas_call x1, Pallas kernels, local(): pl.pallas_call(functools.partial(finish, dims), out_shape=(jax.ShapeDtype...  1.76 us

profile of v3, /device:TPU:1, one launch (start us, length us, event | category | flops | bytes accessed | tf_op | source)
XLA Modules:
  0.0 44.0 jit_solution(4958271264225725510)
XLA Ops:
  0.6 41.6 %wave_ocean.1 = (bf16[2048,512]{1,0:T(8,128)(2,1)S(1)}, f32[2,6,144,128]{3,2,1,0:T(8,128)S(1)}, f32[512,256]{1,0:T(8,128)S(1)}, f32[512,128]{1,0:T(8,128)S(1)}, ...) custom-call(bf16[2048,512]{1,0:T(8,128)(2,1)} %bitcast.6, s32[16,128]{1,0:T(8,128)} %mask_hbm.1, f32[2,512]{1,0:T(2,128)} %cour_hbm.1, ...), custom_call_target="tpu_custom_call" | custom-call | tf_op jit(solution)/shard_map/wave_ocean/pallas_call | solution.py:383
  42.2 1.8 %last_substep.1 = (bf16[2048,512]{1,0:T(8,128)(2,1)}, f32[1024,128]{1,0:T(8,128)}) custom-call(bf16[2048,512]{1,0:T(8,128)(2,1)S(1)} %get-tuple-element.10.wave, f32[2,6,144,128]{3,2,1,0:T(8,128)S(1)} %get-tuple-element.11.last, f32[512,256]{1,0:T(8,128)S(1)} %get-tuple-element.12.stokes, f32[512,128]{1,0:T(8,128)S(1)} %get-tuple-element.13.mask_t, ...), custom_call_target="tpu_custom_call" | custom-call | tf_op jit(solution)/shard_map/last_substep/pallas_call | solution.py:434

commit v4 on v3

--- a/solution.py
+++ b/solution.py
@@ -43,7 +43,7 @@
     spec_hbm, mask_hbm, cour_hbm, inter_hbm, proj_hbm, cur_hbm, drag_hbm,
     wave, last, stokes, mask_t, cor_t, drag_t,
     specx, adv, wmat, proj, projp, maskv, cour, curv, dragv,
-    mask_b, fbuf, ystage, ysend, yrecv, yhalo,
+    mask_b, fbuf, fbuf_n, ystage, ysend, yrecv, yhalo,
     flow, xsend, xrecv, vsend, vrecv,
     load_sem, hx_send, hx_recv, hy_send, hy_recv, av_send, av_recv,
     fx_send, fx_recv, fy_send, fy_recv,
@@ -66,9 +66,10 @@
     def rows(start, count):
         return pl.ds(pl.multiple_of(start * ny, ny), count * ny)
 
-    barrier = pltpu.get_barrier_semaphore()
-    for peer in (west, east, south, north, partner):
-        pl.semaphore_signal(barrier, inc=1, device_id=peer, device_id_type=MESH)
+    with scope("t_sig"):
+        barrier = pltpu.get_barrier_semaphore()
+        for peer in (west, east, south, north, partner):
+            pl.semaphore_signal(barrier, inc=1, device_id=peer, device_id_type=MESH)
 
     loads = []
 
@@ -78,7 +79,14 @@
         loads.append(copy)
         return copy
 
-    spec_load = load(spec_hbm, specx.at[pl.ds(ny, nx * ny), :])
+    def remote(src, dst, send, recv, peer):
+        return pltpu.make_async_remote_copy(
+            src_ref=src, dst_ref=dst, send_sem=send, recv_sem=recv,
+            device_id=peer, device_id_type=MESH,
+        )
+
+    with scope("t_load"):
+        spec_load = load(spec_hbm, specx.at[pl.ds(ny, nx * ny), :])
     cur_load = load(cur_hbm, curv)
     mask_load = load(mask_hbm, maskv)
     cour_load = load(cour_hbm, cour)
@@ -94,22 +102,6 @@
         load(inter_hbm.at[own_k, own_k], wmat.at[pl.ds(0, nk), :]),
         load(inter_hbm.at[oth_k, own_k], wmat.at[pl.ds(nk, nk), :]),
     ]
-
-    def remote(src, dst, send, recv, peer):
-        return pltpu.make_async_remote_copy(
-            src_ref=src, dst_ref=dst, send_sem=send, recv_sem=recv,
-            device_id=peer, device_id_type=MESH,
-        )
-
-    with scope("t_barrier"):
-        pl.semaphore_wait(barrier, 5)
-    hx = [
-        remote(spec_hbm.at[rows(0, 1), :], specx.at[rows(nx + 1, 1), :], hx_send.at[0], hx_recv.at[1], west),
-        remote(spec_hbm.at[rows(nx - 1, 1), :], specx.at[rows(0, 1), :], hx_send.at[1], hx_recv.at[0], east),
-    ]
-    for copy in hx:
-        copy.start()
-
     with scope("t_spec"):
         spec_load.wait()
     for x in range(nx):
@@ -117,12 +109,20 @@
         ystage[0, x:x + 1, :] = specx[first:first + 16, :].astype(F32)[0:1]
         ystage[1, x:x + 1, :] = specx[first + ny - 16:first + ny, :].astype(F32)[15:16]
     ysend[...] = ystage[...].astype(BF16)
+    with scope("t_barrier"):
+        pl.semaphore_wait(barrier, 5)
     hy = [
         remote(ysend.at[0], yrecv.at[1], hy_send.at[0], hy_recv.at[1], south),
         remote(ysend.at[1], yrecv.at[0], hy_send.at[1], hy_recv.at[0], north),
     ]
     for copy in hy:
         copy.start()
+    hx = [
+        remote(spec_hbm.at[rows(0, 1), :], specx.at[rows(nx + 1, 1), :], hx_send.at[0], hx_recv.at[1], west),
+        remote(spec_hbm.at[rows(nx - 1, 1), :], specx.at[rows(0, 1), :], hx_send.at[1], hx_recv.at[0], east),
+    ]
+    for copy in hx:
+        copy.start()
 
     inner = slice(PAD, PAD + ny)
     lane = lax.broadcasted_iota(jnp.int32, (ny, LANES), 1)
@@ -149,6 +149,13 @@
 
     def send_flow(s):
         now = state(s)
+        for c in (0, 1):
+            for i in range(tiles):
+                r = c * tiles + i
+                vsend[s, 0, r:r + 1, :] = now[c, i + 1, PAD:PAD + 1, :]
+                vsend[s, 1, r:r + 1, :] = now[c, i + 1, PAD + ny - 1:PAD + ny, :]
+        for copy in flow_y(s):
+            copy.start()
         for side, tile, group in ((0, 1, 0), (1, tiles, groups - 1)):
             packed = None
             for c in (0, 1):
@@ -156,15 +163,8 @@
                     g = 2 * c + h
                     part = turn(now[c, tile, PAD + h * half:PAD + (h + 1) * half, :], nl * (g - group))
                     packed = part if packed is None else jnp.where(half_lane >= nl * g, part, packed)
-            xsend[s, side] = packed
+            xsend[s, side] = packed.astype(BF16)
         for copy in flow_x(s):
-            copy.start()
-        for c in (0, 1):
-            for i in range(tiles):
-                r = c * tiles + i
-                vsend[s, 0, r:r + 1, :] = now[c, i + 1, PAD:PAD + 1, :]
-                vsend[s, 1, r:r + 1, :] = now[c, i + 1, PAD + ny - 1:PAD + ny, :]
-        for copy in flow_y(s):
             copy.start()
 
     def take_flow(s):
@@ -175,8 +175,8 @@
             for h in (0, 1):
                 g = 2 * c + h
                 rs = slice(PAD + h * half, PAD + (h + 1) * half)
-                from_west = turn(xrecv[s, 0], -nl * g)
-                from_east = turn(xrecv[s, 1], nl * (groups - 1 - g))
+                from_west = turn(xrecv[s, 0].astype(F32), -nl * g)
+                from_east = turn(xrecv[s, 1].astype(F32), nl * (groups - 1 - g))
                 now[c, 0, rs, :] = jnp.where(half_lane < nl, from_west, turn(now[c, tiles, rs, :], nl))
                 now[c, tiles + 1, rs, :] = jnp.where(
                     half_lane >= LANES - nl, from_east, turn(now[c, 1, rs, :], -nl)
@@ -214,63 +214,113 @@
     lat = (gy * ny + lax.broadcasted_iota(jnp.int32, (ny, LANES), 0)).astype(F32)
     cor_t[...] = jnp.sin(jnp.pi * ((lat + 0.5) / (n_gy * ny) - 0.5))
 
-    with scope("t_late"):
-        for copy in proj_load:
-            copy.wait()
-        drag_load.wait()
+    drag_load.wait()
+    drag_t[...] = jnp.broadcast_to(jnp.concatenate([dragv[...]] * groups, axis=1), drag_t.shape)
+
+    def finish_loads():
         for copy in w_load:
             copy.wait()
-    drag = dragv[...]
-    drag_t[...] = jnp.broadcast_to(jnp.concatenate([drag] * groups, axis=1), drag_t.shape)
+
+    for copy in proj_load:
+        copy.wait()
+    proj[2 * nl:LANES, :] = jnp.zeros((LANES - 2 * nl, 2 * nk), BF16)
     for q in range(groups):
         projp[q] = jnp.zeros(projp.shape[1:], BF16)
         for c in (0, 1):
             projp[q, c * LANES + q * nl:c * LANES + (q + 1) * nl, :] = proj[c * nl:(c + 1) * nl, :]
 
     chunks = nk // 128
-    with scope("t_hy"):
-        for copy in hy:
-            copy.wait_recv()
-    for kc in range(chunks):
-        ks = slice(kc * 128, (kc + 1) * 128)
-        yhalo[0, kc] = yrecv[0, :, ks].astype(F32) * not_first
-        yhalo[1, kc] = yrecv[1, :, ks].astype(F32) * not_last
-
-    def swap(x):
+    rim = 16
+
+    def swap(x, first, count, part):
+        rs = pl.ds(pl.multiple_of(x * ny + first, rim), count)
         return remote(
-            adv.at[rows(x, 1), pl.ds(0, nk)], adv.at[rows(x, 1), pl.ds(nk, nk)],
-            av_send.at[x], av_recv.at[x], partner,
+            adv.at[rs, pl.ds(0, nk)], adv.at[rs, pl.ds(nk, nk)],
+            av_send.at[part, x], av_recv.at[part, x], partner,
         )
 
-    def advect(x, carry):
-        mb = mask_b[rows(x, 1), :]
+    def swaps(x, whole):
+        if whole:
+            return [swap(x, 0, ny, 0)]
+        return [swap(x, rim, ny - 2 * rim, 0), swap(x, 0, rim, 1), swap(x, ny - rim, rim, 2)]
+
+    def advect(x, first, count, buf, base):
+        rs = pl.ds(pl.multiple_of(x * ny + first, rim), count)
+        mb = mask_b[rs, :]
+        at = 8 + first - base
         for kc in range(chunks):
             ks = slice(kc * 128, (kc + 1) * 128)
             a, b = cour[0:1, ks], cour[1:2, ks]
             mag_a, mag_b = jnp.abs(a), jnp.abs(b)
-            here = specx[rows(x + 1, 1), ks].astype(F32)
-            fbuf[kc, 8:8 + ny, :] = here
-            fbuf[kc, 7:8, :] = yhalo[0, kc, pl.ds(x, 1), :]
-            fbuf[kc, 8 + ny:9 + ny, :] = yhalo[1, kc, pl.ds(x, 1), :]
-            ux = jnp.where(a > 0, specx[rows(x, 1), ks].astype(F32), specx[rows(x + 2, 1), ks].astype(F32))
-            uy = jnp.where(b > 0, fbuf[kc, 7:7 + ny, :], fbuf[kc, 9:9 + ny, :])
+            here = buf[kc, at:at + count, :]
+            r_w = pl.ds(pl.multiple_of(x * ny + first, rim), count)
+            r_e = pl.ds(pl.multiple_of((x + 2) * ny + first, rim), count)
+            ux = jnp.where(a > 0, specx[r_w, ks].astype(F32), specx[r_e, ks].astype(F32))
+            uy = jnp.where(b > 0, buf[kc, at - 1:at + count - 1, :], buf[kc, at + 1:at + count + 1, :])
             new = (1.0 - mag_a - mag_b) * here + mag_a * ux + mag_b * uy
-            adv[rows(x, 1), ks] = (mb * new).astype(BF16)
-        swap(x).start()
+            adv[rs, ks] = (mb * new).astype(BF16)
+
+    def widen(x, first, count, buf):
+        for kc in range(chunks):
+            ks = slice(kc * 128, (kc + 1) * 128)
+            rs = pl.ds(pl.multiple_of((x + 1) * ny + first, rim), count)
+            buf[kc, 8:8 + count, :] = specx[rs, ks].astype(F32)
+
+    def halo_rows(x, side, row, buf):
+        for kc in range(chunks):
+            buf[kc, row:row + 1, :] = yhalo[side, kc, pl.ds(x, 1), :]
+
+    def advect_middle(x, carry):
+        widen(x, 0, ny, fbuf)
+        advect(x, rim, ny - 2 * rim, fbuf, 0)
+        swap(x, rim, ny - 2 * rim, 0).start()
         return carry
 
-    def drift(q, fresh):
-        for x in range(q * tiles, (q + 1) * tiles):
-            swap(x).wait_recv()
+    def advect_rim(x, carry):
+        widen(x, 0, 2 * rim, fbuf)
+        halo_rows(x, 0, 7, fbuf)
+        advect(x, 0, rim, fbuf, 0)
+        swap(x, 0, rim, 1).start()
+        widen(x, ny - 2 * rim, 2 * rim, fbuf_n)
+        halo_rows(x, 1, 8 + 2 * rim, fbuf_n)
+        advect(x, ny - rim, rim, fbuf_n, ny - 2 * rim)
+        swap(x, ny - rim, rim, 2).start()
+        return carry
+
+    def advect_all(x):
+        widen(x, 0, ny, fbuf)
+        halo_rows(x, 0, 7, fbuf)
+        halo_rows(x, 1, 8 + ny, fbuf)
+        advect(x, 0, ny, fbuf, 0)
+        swap(x, 0, ny, 0).start()
+
+    def drift(x, count, whole, fresh):
+        q, tile = x // tiles, x % tiles
+        for each in range(x, x + count):
+            for copy in swaps(each, whole):
+                copy.wait_recv()
         part = lax.dot_general(
-            adv[rows(q * tiles, tiles), :], projp[q], (((1,), (1,)), ((), ())),
+            adv[rows(x, count), :], projp[q], (((1,), (1,)), ((), ())),
             preferred_element_type=F32,
         )
-        stokes[...] = part if fresh else stokes[...] + part
+        rs = pl.ds(tile * ny, count * ny)
+        stokes[rs, :] = part if fresh else stokes[rs, :] + part
+
+    def drift_row(x):
+        q, tile = x // tiles, x % tiles
+        swap(x, 0, ny, 0).wait_recv()
+        part = lax.dot_general(
+            adv[rows(x, 1), :], proj[...], (((1,), (1,)), ((), ())), preferred_element_type=F32,
+        )
+        mine = (lane >= q * nl) & (lane < (q + 1) * nl)
+        rs = pl.ds(tile * ny, ny)
+        for c in (0, 1):
+            ls = slice(c * LANES, (c + 1) * LANES)
+            stokes[rs, ls] = stokes[rs, ls] + jnp.where(mine, turn(part, nl * (q - c)), 0.0)
 
     drag_row = drag_t[0:1, :]
 
-    def substep(s):
+    def substep(s, which):
         now, then = state(s), state(s + 1)
 
         def store(i, first, block, u_new, v_new):
@@ -282,7 +332,7 @@
             advance(now, stokes, mask_t, cor_t, drag_row, ny, i, store)
             return carry
 
-        lax.fori_loop(0, tiles, one, 0)
+        lax.fori_loop(*which[:2], lambda n, carry: one(which[2] * n, carry), 0)
 
     wide = 256
 
@@ -296,31 +346,50 @@
             wave[rs, ns] = (mb * (adv[rs, ns].astype(F32) + got)).astype(BF16)
         return carry
 
-    with scope("t_advect"):
-        lax.fori_loop(1, nx - 1, advect, 0)
+    with scope("t_middle"):
+        lax.fori_loop(1, nx - 1, advect_middle, 0)
+    with scope("t_hy"):
+        for copy in hy:
+            copy.wait_recv()
+    for kc in range(chunks):
+        ks = slice(kc * 128, (kc + 1) * 128)
+        yhalo[0, kc] = yrecv[0, :, ks].astype(F32) * not_first
+        yhalo[1, kc] = yrecv[1, :, ks].astype(F32) * not_last
+    with scope("t_rim"):
+        lax.fori_loop(1, nx - 1, advect_rim, 0)
+    with scope("t_late"):
+        finish_loads()
+    with scope("t_drift"):
+        for q in range(1, groups - 1):
+            drift(q * tiles, tiles, False, q == 1)
     with scope("t_hx"):
         for copy in hx:
             copy.wait_recv()
     with scope("t_edge"):
-        for x in (0, nx - 1):
-            advect(x, 0)
-    with scope("t_drift"):
-        for n, q in enumerate(list(range(1, groups - 1)) + [0, groups - 1]):
-            drift(q, n == 0)
+        advect_all(0)
+        advect_all(nx - 1)
+    with scope("t_drift3"):
+        drift(1, tiles - 1, False, False)
+        drift(nx - tiles, tiles - 1, False, False)
     with scope("t_take0"):
         take_flow(0)
-    with scope("t_sub0"):
-        substep(0)
+    with scope("t_sub0a"):
+        substep(0, (1, tiles - 1, 1))
+    with scope("t_driftE"):
+        drift_row(0)
+        drift_row(nx - 1)
+    with scope("t_sub0b"):
+        substep(0, (0, 2, tiles - 1))
         send_flow(1)
     with scope("t_gainA"):
-        lax.fori_loop(0, nx // 4 - 1, gain, 0)
+        lax.fori_loop(1, nx // 4, gain, 0)
     with scope("t_take1"):
         take_flow(1)
     with scope("t_sub1"):
-        substep(1)
+        substep(1, (0, tiles, 1))
         send_flow(2)
     with scope("t_gainB"):
-        gain(nx // 4 - 1, 0)
+        gain(0, 0)
     with scope("t_take2"):
         take_flow(2)
 
@@ -332,10 +401,13 @@
                 copy.wait_send()
 
         def drain(x, carry):
-            swap(x).wait_send()
+            for copy in swaps(x, False):
+                copy.wait_send()
             return carry
 
-        lax.fori_loop(0, nx, drain, 0)
+        lax.fori_loop(1, nx - 1, drain, 0)
+        for x in (0, nx - 1):
+            swap(x, 0, ny, 0).wait_send()
 
 
 def finish(
@@ -396,7 +468,7 @@
             pltpu.VMEM(((nx + 2) * ny, nk), BF16),
             pltpu.VMEM((nx * ny, 2 * nk), BF16),
             pltpu.VMEM((2 * nk, nk), BF16),
-            pltpu.VMEM((2 * nl, 2 * nk), BF16),
+            pltpu.VMEM((LANES, 2 * nk), BF16),
             pltpu.VMEM((groups, 2 * LANES, 2 * nk), BF16),
             pltpu.VMEM((nx, ny), jnp.int32),
             pltpu.VMEM((2, nk), F32),
@@ -404,18 +476,19 @@
             pltpu.VMEM((1, nl), F32),
             pltpu.VMEM((nx * ny, 128), F32),
             pltpu.VMEM((nk // 128, ny + 16, 128), F32),
+            pltpu.VMEM((nk // 128, 48, 128), F32),
             pltpu.VMEM((2, nx, nk), F32),
             pltpu.VMEM((2, nx, nk), BF16),
             pltpu.VMEM((2, nx, nk), BF16),
             pltpu.VMEM((2, nk // 128, nx, 128), F32),
             pltpu.VMEM((SUBSTEPS - 1, 2, tiles + 2, ny + 2 * PAD, LANES), F32),
-            pltpu.VMEM((SUBSTEPS, 2, ny // 2, LANES), F32),
-            pltpu.VMEM((SUBSTEPS, 2, ny // 2, LANES), F32),
+            pltpu.VMEM((SUBSTEPS, 2, ny // 2, LANES), BF16),
+            pltpu.VMEM((SUBSTEPS, 2, ny // 2, LANES), BF16),
             pltpu.VMEM((SUBSTEPS, 2, 2 * tiles, LANES), F32),
             pltpu.VMEM((SUBSTEPS, 2, 2 * tiles, LANES), F32),
             dma((12,)),
             dma((2,)), dma((2,)), dma((2,)), dma((2,)),
-            dma((nx,)), dma((nx,)),
+            dma((3, nx)), dma((3, nx)),
             dma((SUBSTEPS, 2)), dma((SUBSTEPS, 2)), dma((SUBSTEPS, 2)), dma((SUBSTEPS, 2)),
         ],
         compiler_params=pltpu.CompilerParams(

time: 44.1 us -> 38.5 us (0.87)
  Pallas kernels: 43.4 us -> 37.7 us
    pallas_call x1, Pallas kernels: 41.6 us -> 36 us  [local(): pl.pallas_call(functools.partial(kernel, dims), out_shape=(jax.ShapeDtype...]
where the time goes in v4:
time: 38.5 us; the launch traced here: 38.4 us
  Pallas kernels  37.7 us (98%)
  between operations  0.64 us (2%)
    pallas_call x1, Pallas kernels, local(): pl.pallas_call(functools.partial(kernel, dims), out_shape=(jax.ShapeDtype...  36 us
    pallas_call x1, Pallas kernels, local(): pl.pallas_call(functools.partial(finish, dims), out_shape=(jax.ShapeDtype...  1.76 us

profile of v4, /device:TPU:1, one launch (start us, length us, event | category | flops | bytes accessed | tf_op | source)
XLA Modules:
  0.0 38.4 jit_solution(10007030603196668862)
XLA Ops:
  0.6 36.0 %wave_ocean.1 = (bf16[2048,512]{1,0:T(8,128)(2,1)S(1)}, f32[2,6,144,128]{3,2,1,0:T(8,128)S(1)}, f32[512,256]{1,0:T(8,128)S(1)}, f32[512,128]{1,0:T(8,128)S(1)}, ...) custom-call(bf16[2048,512]{1,0:T(8,128)(2,1)} %bitcast.6, s32[16,128]{1,0:T(8,128)} %mask_hbm.1, f32[2,512]{1,0:T(2,128)} %cour_hbm.1, ...), custom_call_target="tpu_custom_call" | custom-call | tf_op jit(solution)/shard_map/wave_ocean/pallas_call | solution.py:455
  36.6 1.8 %last_substep.1 = (bf16[2048,512]{1,0:T(8,128)(2,1)}, f32[1024,128]{1,0:T(8,128)}) custom-call(bf16[2048,512]{1,0:T(8,128)(2,1)S(1)} %get-tuple-element.10.wave, f32[2,6,144,128]{3,2,1,0:T(8,128)S(1)} %get-tuple-element.11.last, f32[512,256]{1,0:T(8,128)S(1)} %get-tuple-element.12.stokes, f32[512,128]{1,0:T(8,128)S(1)} %get-tuple-element.13.mask_t, ...), custom_call_target="tpu_custom_call" | custom-call | tf_op jit(solution)/shard_map/last_substep/pallas_call | solution.py:507

commit v5 on v4

--- a/solution.py
+++ b/solution.py
@@ -85,11 +85,16 @@
             device_id=peer, device_id_type=MESH,
         )
 
-    with scope("t_load"):
-        spec_load = load(spec_hbm, specx.at[pl.ds(ny, nx * ny), :])
+    rim = 16
+    rim_load = [
+        load(spec_hbm.at[:, pl.ds(first, rim), :], specx.at[pl.ds(1, nx), pl.ds(first, rim), :])
+        for first in (0, ny - rim)
+    ]
     cur_load = load(cur_hbm, curv)
     mask_load = load(mask_hbm, maskv)
     cour_load = load(cour_hbm, cour)
+    middle = pl.ds(rim, ny - 2 * rim)
+    spec_load = load(spec_hbm.at[:, middle, :], specx.at[pl.ds(1, nx), middle, :])
     own_k = pl.ds(pl.multiple_of(core * nk, nk), nk)
     oth_k = pl.ds(pl.multiple_of(other * nk, nk), nk)
     own_l = pl.ds(pl.multiple_of(core * nl, nl), nl)
@@ -103,11 +108,11 @@
         load(inter_hbm.at[oth_k, own_k], wmat.at[pl.ds(nk, nk), :]),
     ]
     with scope("t_spec"):
-        spec_load.wait()
+        for copy in rim_load:
+            copy.wait()
     for x in range(nx):
-        first = (1 + x) * ny
-        ystage[0, x:x + 1, :] = specx[first:first + 16, :].astype(F32)[0:1]
-        ystage[1, x:x + 1, :] = specx[first + ny - 16:first + ny, :].astype(F32)[15:16]
+        ystage[0, x:x + 1, :] = specx[1 + x, 0:rim, :].astype(F32)[0:1]
+        ystage[1, x:x + 1, :] = specx[1 + x, ny - rim:ny, :].astype(F32)[rim - 1:rim]
     ysend[...] = ystage[...].astype(BF16)
     with scope("t_barrier"):
         pl.semaphore_wait(barrier, 5)
@@ -117,12 +122,19 @@
     ]
     for copy in hy:
         copy.start()
-    hx = [
-        remote(spec_hbm.at[rows(0, 1), :], specx.at[rows(nx + 1, 1), :], hx_send.at[0], hx_recv.at[1], west),
-        remote(spec_hbm.at[rows(nx - 1, 1), :], specx.at[rows(0, 1), :], hx_send.at[1], hx_recv.at[0], east),
-    ]
-    for copy in hx:
-        copy.start()
+    def edge_of(n):
+        return lax.rem(lax.rem(gx, 2) + n, 2)
+
+    def hx(n):
+        f = edge_of(n)
+        peer = (lax.rem(gx + n_gx - 1 + 2 * f, n_gx), gy, core)
+        return remote(
+            spec_hbm.at[f * (nx - 1)], specx.at[(1 - f) * (nx + 1)],
+            hx_send.at[n], hx_recv.at[n], peer,
+        )
+
+    for n in (0, 1):
+        hx(n).start()
 
     inner = slice(PAD, PAD + ny)
     lane = lax.broadcasted_iota(jnp.int32, (ny, LANES), 1)
@@ -230,7 +242,6 @@
             projp[q, c * LANES + q * nl:c * LANES + (q + 1) * nl, :] = proj[c * nl:(c + 1) * nl, :]
 
     chunks = nk // 128
-    rim = 16
 
     def swap(x, first, count, part):
         rs = pl.ds(pl.multiple_of(x * ny + first, rim), count)
@@ -239,9 +250,7 @@
             av_send.at[part, x], av_recv.at[part, x], partner,
         )
 
-    def swaps(x, whole):
-        if whole:
-            return [swap(x, 0, ny, 0)]
+    def swaps(x):
         return [swap(x, rim, ny - 2 * rim, 0), swap(x, 0, rim, 1), swap(x, ny - rim, rim, 2)]
 
     def advect(x, first, count, buf, base):
@@ -253,9 +262,8 @@
             a, b = cour[0:1, ks], cour[1:2, ks]
             mag_a, mag_b = jnp.abs(a), jnp.abs(b)
             here = buf[kc, at:at + count, :]
-            r_w = pl.ds(pl.multiple_of(x * ny + first, rim), count)
-            r_e = pl.ds(pl.multiple_of((x + 2) * ny + first, rim), count)
-            ux = jnp.where(a > 0, specx[r_w, ks].astype(F32), specx[r_e, ks].astype(F32))
+            ys = slice(first, first + count)
+            ux = jnp.where(a > 0, specx[x, ys, ks].astype(F32), specx[x + 2, ys, ks].astype(F32))
             uy = jnp.where(b > 0, buf[kc, at - 1:at + count - 1, :], buf[kc, at + 1:at + count + 1, :])
             new = (1.0 - mag_a - mag_b) * here + mag_a * ux + mag_b * uy
             adv[rs, ks] = (mb * new).astype(BF16)
@@ -263,8 +271,7 @@
     def widen(x, first, count, buf):
         for kc in range(chunks):
             ks = slice(kc * 128, (kc + 1) * 128)
-            rs = pl.ds(pl.multiple_of((x + 1) * ny + first, rim), count)
-            buf[kc, 8:8 + count, :] = specx[rs, ks].astype(F32)
+            buf[kc, 8:8 + count, :] = specx[x + 1, first:first + count, ks].astype(F32)
 
     def halo_rows(x, side, row, buf):
         for kc in range(chunks):
@@ -287,17 +294,20 @@
         swap(x, ny - rim, rim, 2).start()
         return carry
 
-    def advect_all(x):
+    def advect_edge(n, carry):
+        hx(n).wait_recv()
+        x = edge_of(n) * (nx - 1)
         widen(x, 0, ny, fbuf)
         halo_rows(x, 0, 7, fbuf)
         halo_rows(x, 1, 8 + ny, fbuf)
         advect(x, 0, ny, fbuf, 0)
         swap(x, 0, ny, 0).start()
-
-    def drift(x, count, whole, fresh):
+        return carry
+
+    def drift(x, count, fresh):
         q, tile = x // tiles, x % tiles
         for each in range(x, x + count):
-            for copy in swaps(each, whole):
+            for copy in swaps(each):
                 copy.wait_recv()
         part = lax.dot_general(
             adv[rows(x, count), :], projp[q], (((1,), (1,)), ((), ())),
@@ -306,21 +316,24 @@
         rs = pl.ds(tile * ny, count * ny)
         stokes[rs, :] = part if fresh else stokes[rs, :] + part
 
-    def drift_row(x):
-        q, tile = x // tiles, x % tiles
+    def drift_row(n, carry):
+        f = edge_of(n)
+        x, q, tile = f * (nx - 1), f * (groups - 1), f * (tiles - 1)
         swap(x, 0, ny, 0).wait_recv()
         part = lax.dot_general(
             adv[rows(x, 1), :], proj[...], (((1,), (1,)), ((), ())), preferred_element_type=F32,
         )
         mine = (lane >= q * nl) & (lane < (q + 1) * nl)
-        rs = pl.ds(tile * ny, ny)
+        rs = rows(tile, 1)
         for c in (0, 1):
             ls = slice(c * LANES, (c + 1) * LANES)
-            stokes[rs, ls] = stokes[rs, ls] + jnp.where(mine, turn(part, nl * (q - c)), 0.0)
+            moved = pltpu.roll(part, lax.rem(nl * q + LANES - nl * c, LANES), 1)
+            stokes[rs, ls] = stokes[rs, ls] + jnp.where(mine, moved, 0.0)
+        return carry
 
     drag_row = drag_t[0:1, :]
 
-    def substep(s, which):
+    def substep(s):
         now, then = state(s), state(s + 1)
 
         def store(i, first, block, u_new, v_new):
@@ -332,7 +345,7 @@
             advance(now, stokes, mask_t, cor_t, drag_row, ny, i, store)
             return carry
 
-        lax.fori_loop(*which[:2], lambda n, carry: one(which[2] * n, carry), 0)
+        lax.fori_loop(0, tiles, one, 0)
 
     wide = 256
 
@@ -346,6 +359,7 @@
             wave[rs, ns] = (mb * (adv[rs, ns].astype(F32) + got)).astype(BF16)
         return carry
 
+    spec_load.wait()
     with scope("t_middle"):
         lax.fori_loop(1, nx - 1, advect_middle, 0)
     with scope("t_hy"):
@@ -361,32 +375,24 @@
         finish_loads()
     with scope("t_drift"):
         for q in range(1, groups - 1):
-            drift(q * tiles, tiles, False, q == 1)
+            drift(q * tiles, tiles, q == 1)
+        drift(1, tiles - 1, False)
+        drift(nx - tiles, tiles - 1, False)
     with scope("t_hx"):
-        for copy in hx:
-            copy.wait_recv()
-    with scope("t_edge"):
-        advect_all(0)
-        advect_all(nx - 1)
-    with scope("t_drift3"):
-        drift(1, tiles - 1, False, False)
-        drift(nx - tiles, tiles - 1, False, False)
+        lax.fori_loop(0, 2, advect_edge, 0)
+    with scope("t_driftE"):
+        lax.fori_loop(0, 2, drift_row, 0)
     with scope("t_take0"):
         take_flow(0)
-    with scope("t_sub0a"):
-        substep(0, (1, tiles - 1, 1))
-    with scope("t_driftE"):
-        drift_row(0)
-        drift_row(nx - 1)
-    with scope("t_sub0b"):
-        substep(0, (0, 2, tiles - 1))
+    with scope("t_sub0"):
+        substep(0)
         send_flow(1)
     with scope("t_gainA"):
         lax.fori_loop(1, nx // 4, gain, 0)
     with scope("t_take1"):
         take_flow(1)
     with scope("t_sub1"):
-        substep(1, (0, tiles, 1))
+        substep(1)
         send_flow(2)
     with scope("t_gainB"):
         gain(0, 0)
@@ -394,14 +400,14 @@
         take_flow(2)
 
     with scope("t_out"):
-        for copy in hy + hx:
+        for copy in hy + [hx(0), hx(1)]:
             copy.wait_send()
         for s in range(SUBSTEPS):
             for copy in flow_x(s) + flow_y(s):
                 copy.wait_send()
 
         def drain(x, carry):
-            for copy in swaps(x, False):
+            for copy in swaps(x):
                 copy.wait_send()
             return carry
 
@@ -465,7 +471,7 @@
         in_specs=[hbm] * 7,
         out_specs=(vmem,) * 6,
         scratch_shapes=[
-            pltpu.VMEM(((nx + 2) * ny, nk), BF16),
+            pltpu.VMEM((nx + 2, ny, nk), BF16),
             pltpu.VMEM((nx * ny, 2 * nk), BF16),
             pltpu.VMEM((2 * nk, nk), BF16),
             pltpu.VMEM((LANES, 2 * nk), BF16),
@@ -486,7 +492,7 @@
             pltpu.VMEM((SUBSTEPS, 2, ny // 2, LANES), BF16),
             pltpu.VMEM((SUBSTEPS, 2, 2 * tiles, LANES), F32),
             pltpu.VMEM((SUBSTEPS, 2, 2 * tiles, LANES), F32),
-            dma((12,)),
+            dma((14,)),
             dma((2,)), dma((2,)), dma((2,)), dma((2,)),
             dma((3, nx)), dma((3, nx)),
             dma((SUBSTEPS, 2)), dma((SUBSTEPS, 2)), dma((SUBSTEPS, 2)), dma((SUBSTEPS, 2)),
@@ -496,7 +502,7 @@
         ),
         name="wave_ocean",
     )(*(pltpu.with_memory_space_constraint(each, pltpu.HBM) for each in (
-        spectrum.reshape(nx * ny, nk),
+        spectrum,
         sea_mask,
         courant,
         interaction,

time: 38.5 us -> 38 us (0.987)
  Pallas kernels: 37.7 us -> 37.3 us
    pallas_call x1, Pallas kernels: 36 us -> 35.5 us  [local(): pl.pallas_call(functools.partial(kernel, dims), out_shape=(jax.ShapeDtype...]
where the time goes in v5:
time: 38 us; the launch traced here: 37.9 us
  Pallas kernels  37.3 us (98%)
  between operations  0.64 us (2%)
    pallas_call x1, Pallas kernels, local(): pl.pallas_call(functools.partial(kernel, dims), out_shape=(jax.ShapeDtype...  35.5 us
    pallas_call x1, Pallas kernels, local(): pl.pallas_call(functools.partial(finish, dims), out_shape=(jax.ShapeDtype...  1.76 us

profile of v5, /device:TPU:1, one launch (start us, length us, event | category | flops | bytes accessed | tf_op | source)
XLA Modules:
  0.0 37.9 jit_solution(3950899345483572087)
XLA Ops:
  0.6 35.5 %wave_ocean.1 = (bf16[2048,512]{1,0:T(8,128)(2,1)S(1)}, f32[2,6,144,128]{3,2,1,0:T(8,128)S(1)}, f32[512,256]{1,0:T(8,128)S(1)}, f32[512,128]{1,0:T(8,128)S(1)}, ...) custom-call(bf16[16,128,512]{2,1,0:T(8,128)(2,1)} %spec_hbm.1, s32[16,128]{1,0:T(8,128)} %mask_hbm.1, f32[2,512]{1,0:T(2,128)} %cour_hbm.1, ...), custom_call_target="tpu_custom_call" | custom-call | tf_op jit(solution)/shard_map/wave_ocean/pallas_call | solution.py:461
  36.2 1.8 %last_substep.1 = (bf16[2048,512]{1,0:T(8,128)(2,1)}, f32[1024,128]{1,0:T(8,128)}) custom-call(bf16[2048,512]{1,0:T(8,128)(2,1)S(1)} %get-tuple-element.10.wave, f32[2,6,144,128]{3,2,1,0:T(8,128)S(1)} %get-tuple-element.11.last, f32[512,256]{1,0:T(8,128)S(1)} %get-tuple-element.12.stokes, f32[512,128]{1,0:T(8,128)S(1)} %get-tuple-element.13.mask_t, ...), custom_call_target="tpu_custom_call" | custom-call | tf_op jit(solution)/shard_map/last_substep/pallas_call | solution.py:513

commit v6 on v5

--- a/solution.py
+++ b/solution.py
@@ -19,9 +19,12 @@
 LANES = 128
 
 
-def advance(flow, stokes, mask_t, cor_t, drag, ny, i, store):
-    block = 32
-    for first in range(0, ny, block):
+BLOCK = 32
+
+
+def advance(flow, stokes, mask_t, cor_t, drag, ny, i, firsts, store):
+    block = BLOCK
+    for first in firsts:
         at = PAD + first
         u, v = (flow[c, i + 1, at:at + block, :] for c in (0, 1))
         u_w, v_w = (flow[c, i, at:at + block, :] for c in (0, 1))
@@ -159,7 +162,7 @@
     def turn(q, lanes):
         return pltpu.roll(q, lanes % LANES, 1) if lanes % LANES else q
 
-    def send_flow(s):
+    def send_flow_y(s):
         now = state(s)
         for c in (0, 1):
             for i in range(tiles):
@@ -168,6 +171,9 @@
                 vsend[s, 1, r:r + 1, :] = now[c, i + 1, PAD + ny - 1:PAD + ny, :]
         for copy in flow_y(s):
             copy.start()
+
+    def send_flow_x(s):
+        now = state(s)
         for side, tile, group in ((0, 1, 0), (1, tiles, groups - 1)):
             packed = None
             for c in (0, 1):
@@ -209,7 +215,8 @@
                 [curv[pl.ds(c * nl * nx + q * tiles + i, nl, stride=nx), :] for q in range(groups)], axis=0
             )
             flow[0, c, i + 1, inner, :] = tile.T
-    send_flow(0)
+    send_flow_y(0)
+    send_flow_x(0)
 
     mask_load.wait()
     cour_load.wait()
@@ -341,11 +348,17 @@
             then[0, i + 1, at, :] = u_new
             then[1, i + 1, at, :] = v_new
 
-        def one(i, carry):
-            advance(now, stokes, mask_t, cor_t, drag_row, ny, i, store)
-            return carry
-
-        lax.fori_loop(0, tiles, one, 0)
+        def some(firsts):
+            def one(i, carry):
+                advance(now, stokes, mask_t, cor_t, drag_row, ny, i, firsts, store)
+                return carry
+
+            lax.fori_loop(0, tiles, one, 0)
+
+        some((0, ny - BLOCK))
+        send_flow_y(s + 1)
+        some(tuple(range(BLOCK, ny - BLOCK, BLOCK)))
+        send_flow_x(s + 1)
 
     wide = 256
 
@@ -377,25 +390,25 @@
         for q in range(1, groups - 1):
             drift(q * tiles, tiles, q == 1)
         drift(1, tiles - 1, False)
-        drift(nx - tiles, tiles - 1, False)
     with scope("t_hx"):
         lax.fori_loop(0, 2, advect_edge, 0)
+    with scope("t_drift3"):
+        drift(nx - tiles, tiles - 1, False)
     with scope("t_driftE"):
         lax.fori_loop(0, 2, drift_row, 0)
     with scope("t_take0"):
         take_flow(0)
     with scope("t_sub0"):
         substep(0)
-        send_flow(1)
     with scope("t_gainA"):
-        lax.fori_loop(1, nx // 4, gain, 0)
+        lax.fori_loop(1, nx // 8 + 1, gain, 0)
     with scope("t_take1"):
         take_flow(1)
     with scope("t_sub1"):
         substep(1)
-        send_flow(2)
     with scope("t_gainB"):
-        gain(0, 0)
+        for p in [0] + list(range(nx // 8 + 1, nx // 4)):
+            gain(p, 0)
     with scope("t_take2"):
         take_flow(2)
 
@@ -435,7 +448,7 @@
 
     puts = [put]
     for i in range(tiles):
-        advance(last, stokes, mask_t, cor_t, drag_row, ny, i, store)
+        advance(last, stokes, mask_t, cor_t, drag_row, ny, i, range(0, ny, BLOCK), store)
     for c in (0, 1):
         for i in range(tiles):
             tile = done[c, i].T

time: 38 us -> 37.5 us (0.987)
  Pallas kernels: 37.3 us -> 36.7 us
    pallas_call x1, Pallas kernels: 35.5 us -> 34.9 us  [local(): pl.pallas_call(functools.partial(kernel, dims), out_shape=(jax.ShapeDtype...]
where the time goes in v6:
time: 37.5 us; the launch traced here: 37.3 us
  Pallas kernels  36.7 us (98%)
  between operations  0.64 us (2%)
    pallas_call x1, Pallas kernels, local(): pl.pallas_call(functools.partial(kernel, dims), out_shape=(jax.ShapeDtype...  34.9 us
    pallas_call x1, Pallas kernels, local(): pl.pallas_call(functools.partial(finish, dims), out_shape=(jax.ShapeDtype...  1.76 us

profile of v6, /device:TPU:1, one launch (start us, length us, event | category | flops | bytes accessed | tf_op | source)
XLA Modules:
  0.0 37.3 jit_solution(13307839293871220359)
XLA Ops:
  0.6 34.9 %wave_ocean.1 = (bf16[2048,512]{1,0:T(8,128)(2,1)S(1)}, f32[2,6,144,128]{3,2,1,0:T(8,128)S(1)}, f32[512,256]{1,0:T(8,128)S(1)}, f32[512,128]{1,0:T(8,128)S(1)}, ...) custom-call(bf16[16,128,512]{2,1,0:T(8,128)(2,1)} %spec_hbm.1, s32[16,128]{1,0:T(8,128)} %mask_hbm.1, f32[2,512]{1,0:T(2,128)} %cour_hbm.1, ...), custom_call_target="tpu_custom_call" | custom-call | tf_op jit(solution)/shard_map/wave_ocean/pallas_call | solution.py:474
  35.6 1.8 %last_substep.1 = (bf16[2048,512]{1,0:T(8,128)(2,1)}, f32[1024,128]{1,0:T(8,128)}) custom-call(bf16[2048,512]{1,0:T(8,128)(2,1)S(1)} %get-tuple-element.10.wave, f32[2,6,144,128]{3,2,1,0:T(8,128)S(1)} %get-tuple-element.11.last, f32[512,256]{1,0:T(8,128)S(1)} %get-tuple-element.12.stokes, f32[512,128]{1,0:T(8,128)S(1)} %get-tuple-element.13.mask_t, ...), custom_call_target="tpu_custom_call" | custom-call | tf_op jit(solution)/shard_map/last_substep/pallas_call | solution.py:526

commit v7 on v6

--- a/solution.py
+++ b/solution.py
@@ -185,7 +185,7 @@
         for copy in flow_x(s):
             copy.start()
 
-    def take_flow(s):
+    def take_flow_x(s):
         now = state(s)
         for copy in flow_x(s):
             copy.wait_recv()
@@ -199,6 +199,9 @@
                 now[c, tiles + 1, rs, :] = jnp.where(
                     half_lane >= LANES - nl, from_east, turn(now[c, 1, rs, :], -nl)
                 )
+
+    def take_flow_y(s):
+        now = state(s)
         for copy in flow_y(s):
             copy.wait_recv()
         for c in (0, 1):
@@ -348,17 +351,17 @@
             then[0, i + 1, at, :] = u_new
             then[1, i + 1, at, :] = v_new
 
-        def some(firsts):
-            def one(i, carry):
-                advance(now, stokes, mask_t, cor_t, drag_row, ny, i, firsts, store)
+        def some(count, tile, firsts):
+            def one(n, carry):
+                advance(now, stokes, mask_t, cor_t, drag_row, ny, tile(n), firsts, store)
                 return carry
 
-            lax.fori_loop(0, tiles, one, 0)
-
-        some((0, ny - BLOCK))
-        send_flow_y(s + 1)
-        some(tuple(range(BLOCK, ny - BLOCK, BLOCK)))
-        send_flow_x(s + 1)
+            lax.fori_loop(0, count, one, 0)
+
+        return some
+
+    edge_blocks = (0, ny - BLOCK)
+    inner_blocks = tuple(range(BLOCK, ny - BLOCK, BLOCK))
 
     wide = 256
 
@@ -394,23 +397,37 @@
         lax.fori_loop(0, 2, advect_edge, 0)
     with scope("t_drift3"):
         drift(nx - tiles, tiles - 1, False)
+    with scope("t_take0y"):
+        take_flow_y(0)
+    some = substep(0)
+    with scope("t_sub0a"):
+        some(tiles - 2, lambda n: n + 1, edge_blocks + inner_blocks)
     with scope("t_driftE"):
         lax.fori_loop(0, 2, drift_row, 0)
-    with scope("t_take0"):
-        take_flow(0)
+    with scope("t_take0x"):
+        take_flow_x(0)
     with scope("t_sub0"):
-        substep(0)
+        some(2, lambda n: n * (tiles - 1), edge_blocks)
+        send_flow_y(1)
+        some(2, lambda n: n * (tiles - 1), inner_blocks)
+        send_flow_x(1)
     with scope("t_gainA"):
         lax.fori_loop(1, nx // 8 + 1, gain, 0)
     with scope("t_take1"):
-        take_flow(1)
+        take_flow_x(1)
+        take_flow_y(1)
     with scope("t_sub1"):
-        substep(1)
+        some = substep(1)
+        some(tiles, lambda n: n, edge_blocks)
+        send_flow_y(2)
+        some(tiles, lambda n: n, inner_blocks)
+        send_flow_x(2)
     with scope("t_gainB"):
         for p in [0] + list(range(nx // 8 + 1, nx // 4)):
             gain(p, 0)
     with scope("t_take2"):
-        take_flow(2)
+        take_flow_x(2)
+        take_flow_y(2)
 
     with scope("t_out"):
         for copy in hy + [hx(0), hx(1)]:
@@ -438,28 +455,37 @@
     nx, ny, nk, nl = dims
     groups = LANES // nl
     tiles = nx // groups
-    put = pltpu.make_async_copy(wave, wave_hbm, out_sem.at[0])
-    put.start()
+    puts = []
+
+    def put(src, dst):
+        copy = pltpu.make_async_copy(src, dst, out_sem.at[len(puts)])
+        copy.start()
+        puts.append(copy)
+
+    count = nx * ny // 4
+    for n in range(4):
+        part = pl.ds(n * count, count)
+        put(wave.at[part, :], wave_hbm.at[part, :])
     drag_row = drag_t[0:1, :]
 
     def store(i, first, block, u_new, v_new):
         done[0, i, first:first + block, :] = u_new
         done[1, i, first:first + block, :] = v_new
 
-    puts = [put]
-    for i in range(tiles):
+    def one(i, carry):
         advance(last, stokes, mask_t, cor_t, drag_row, ny, i, range(0, ny, BLOCK), store)
+        return carry
+
+    lax.fori_loop(0, tiles, one, 0)
     for c in (0, 1):
         for i in range(tiles):
             tile = done[c, i].T
             for q in range(groups):
                 coutv[pl.ds(c * nl * nx + q * tiles + i, nl, stride=nx), :] = tile[q * nl:(q + 1) * nl]
         part = pl.ds(c * nl * nx, nl * nx)
-        put = pltpu.make_async_copy(coutv.at[part, :], curo_hbm.at[part, :], out_sem.at[1 + c])
-        put.start()
-        puts.append(put)
-    for put in puts:
-        put.wait()
+        put(coutv.at[part, :], curo_hbm.at[part, :])
+    for copy in puts:
+        copy.wait()
 
 
 def local(spectrum, sea_mask, courant, interaction, stokes_proj, currents, level_drag):
@@ -534,7 +560,7 @@
         scratch_shapes=[
             pltpu.VMEM((2, tiles, ny, LANES), F32),
             pltpu.VMEM((2 * nl * nx, ny), F32),
-            dma((3,)),
+            dma((6,)),
         ],
         compiler_params=pltpu.CompilerParams(vmem_limit_bytes=40 * 1024 * 1024),
         name="last_substep",

time: 37.5 us -> 37.2 us (level)
  no operation moved by 1% of the time
where the time goes in v7:
time: 37.2 us; the launch traced here: 37.1 us
  Pallas kernels  36.5 us (98%)
  between operations  0.64 us (2%)
    pallas_call x1, Pallas kernels, local(): pl.pallas_call(functools.partial(kernel, dims), out_shape=(jax.ShapeDtype...  34.9 us
    pallas_call x1, Pallas kernels, local(): pl.pallas_call(functools.partial(finish, dims), out_shape=(jax.ShapeDtype...  1.53 us

profile of v7, /device:TPU:1, one launch (start us, length us, event | category | flops | bytes accessed | tf_op | source)
XLA Modules:
  0.0 37.1 jit_solution(941850841248191375)
XLA Ops:
  0.6 34.9 %wave_ocean.1 = (bf16[2048,512]{1,0:T(8,128)(2,1)S(1)}, f32[2,6,144,128]{3,2,1,0:T(8,128)S(1)}, f32[512,256]{1,0:T(8,128)S(1)}, f32[512,128]{1,0:T(8,128)S(1)}, ...) custom-call(bf16[16,128,512]{2,1,0:T(8,128)(2,1)} %spec_hbm.1, s32[16,128]{1,0:T(8,128)} %mask_hbm.1, f32[2,512]{1,0:T(2,128)} %cour_hbm.1, ...), custom_call_target="tpu_custom_call" | custom-call | tf_op jit(solution)/shard_map/wave_ocean/pallas_call | solution.py:500
  35.6 1.5 %last_substep.1 = (bf16[2048,512]{1,0:T(8,128)(2,1)}, f32[1024,128]{1,0:T(8,128)}) custom-call(bf16[2048,512]{1,0:T(8,128)(2,1)S(1)} %get-tuple-element.10.wave, f32[2,6,144,128]{3,2,1,0:T(8,128)S(1)} %get-tuple-element.11.last, f32[512,256]{1,0:T(8,128)S(1)} %get-tuple-element.12.stokes, f32[512,128]{1,0:T(8,128)S(1)} %get-tuple-element.13.mask_t, ...), custom_call_target="tpu_custom_call" | custom-call | tf_op jit(solution)/shard_map/last_substep/pallas_call | solution.py:552
